TPU v7x, 32 devices: a whole 2x2x4 slice. The times are simulated.
32 devices in a mesh: slab: 4 (over y, x), block: 8 (over z, core).
Axes of the slice: x: 2, y: 2, z: 4, core: 2. Of those that a mesh axis runs over, the one named last changes fastest.
Arguments:
- lanczos_vector: float32 [3, 32, 64, 256], P(None, 'slab', 'block'), may hold values from -200 to 200
- previous_vector: float32 [3, 32, 64, 256], P(None, 'slab', 'block'), may hold values from -30 to 30
- previous_beta: float32 [], replicated, may hold values from 0.3 to 1
- locked_vectors: float32 [16, 3, 32, 64, 256], P(None, None, 'slab', 'block'), may hold values from -0.0039867997 to 0.0039867997
- occupancy: int32 [4, 8, 32], P('slab', 'block'), may hold values 0 or 1
- young: float32 [32, 64, 256], P('slab', 'block'), may hold values from 0.5 to 4
- couplings: float32 [13, 3, 3], replicated, may hold values from -1 to 1, as said below
- coarse_inverse: float32 [96, 96], P(('slab', 'block')), may hold values from -45 to 165, as said below
Outputs:
- remainder: float32 [3, 32, 64, 256], P(None, 'slab', 'block')
- coefficients: float32 [2], replicated
- projections: float32 [16], replicated
Inputs may be any that keep to these rules, and one draw needn't show every extreme that they name: `couplings`: each block is symmetric and positive definite, with positive diagonal larger than the sum of its off-diagonal magnitudes. `coarse_inverse`: symmetric and positive definite.
All inputs are finite; a program needn't handle non-finite values. No bound on the sum of `occupancy` on one device may be relied on, other than what follows from the above.
Results may differ from a plain program's by a relative error of at most 0.0003.
Values sent between devices are 32-bit elements; how exact they have to be, the bound alone decides.
No kernel may reach another device: no remote copies, remote signals or barrier semaphores. Data moves between devices by JAX's collectives and lax.ppermute only.
A program may use at most 128 MiB of HBM per device.

v0:
```python
import jax
import jax.numpy as jnp
from jax import lax
from jax.sharding import PartitionSpec as P

BRICK = 8
ITERS = 3


SHIFT_MASS = 0.02
SMOOTH_WEIGHT = 0.5
VOID_DENSITY = 0.1
HIGHEST_PRECISION = lax.Precision.HIGHEST


def with_halo(block, sides, width):
    for axis, dim in sides:
        count = lax.axis_size(axis)
        forward = [(i, i + 1) for i in range(count - 1)]
        backward = [(target, source) for source, target in forward]
        low = lax.ppermute(
            lax.slice_in_dim(block, block.shape[dim] - width, None, axis=dim), axis, forward
        )
        high = lax.ppermute(lax.slice_in_dim(block, 0, width, axis=dim), axis, backward)
        block = jnp.concatenate([low, block, high], axis=dim)
    return block


def offset_list():
    offsets = []
    for step_x in (-1, 0, 1):
        for step_y in (-1, 0, 1):
            for step_z in (-1, 0, 1):
                offsets.append((step_x, step_y, step_z))
    return offsets


def pair_block(couplings, number):
    if number < 13:
        return couplings[number]
    return couplings[26 - number]


def operate_padded(vector_field, padded_weighted, padded_root, stiffness, root_stiff, couplings):
    span_x, span_y, span_z = (vector_field.shape[1], vector_field.shape[2], vector_field.shape[3])
    accumulate = jnp.zeros_like(vector_field)
    for number, (step_x, step_y, step_z) in enumerate(offset_list()):
        if number == 13:
            continue
        matrix_pair = pair_block(couplings, number)
        root_near = padded_root[
            1 + step_x : 1 + step_x + span_x,
            1 + step_y : 1 + step_y + span_y,
            1 + step_z : 1 + step_z + span_z,
        ]
        weighted_near = padded_weighted[
            :,
            1 + step_x : 1 + step_x + span_x,
            1 + step_y : 1 + step_y + span_y,
            1 + step_z : 1 + step_z + span_z,
        ]
        differ = root_near[None] * vector_field - weighted_near
        for column in range(3):
            accumulate = (
                accumulate + matrix_pair[:, column][:, None, None, None] * differ[column][None]
            )
    return SHIFT_MASS * stiffness[None] * vector_field + root_stiff[None] * accumulate


def diagonal_of(padded_root, stiffness, root_stiff, couplings):
    span_x, span_y, span_z = stiffness.shape
    accumulate = jnp.zeros((3, span_x, span_y, span_z), jnp.float32)
    for number, (step_x, step_y, step_z) in enumerate(offset_list()):
        if number == 13:
            continue
        matrix_pair = pair_block(couplings, number)
        root_near = padded_root[
            1 + step_x : 1 + step_x + span_x,
            1 + step_y : 1 + step_y + span_y,
            1 + step_z : 1 + step_z + span_z,
        ]
        accumulate = accumulate + jnp.diagonal(matrix_pair)[:, None, None, None] * root_near[None]
    return SHIFT_MASS * stiffness[None] + root_stiff[None] * accumulate


def shards(
    lanczos_vector,
    previous_vector,
    previous_beta,
    locked_vectors,
    occupancy,
    young,
    couplings,
    coarse_inverse,
):
    density = jnp.where(occupancy == 1, 1.0, VOID_DENSITY).astype(jnp.float32)
    density = jnp.repeat(jnp.repeat(jnp.repeat(density, BRICK, 0), BRICK, 1), BRICK, 2)
    stiffness = density * young
    root_stiff = jnp.sqrt(stiffness)
    root_edges = with_halo(root_stiff, (("slab", 0), ("block", 1)), 1)
    padded_root = jnp.pad(root_edges, ((0, 0), (0, 0), (1, 1)))
    diagonal = diagonal_of(padded_root, stiffness, root_stiff, couplings)
    span_x, span_y, span_z = stiffness.shape
    slab_count = lax.axis_size("slab")
    block_count = lax.axis_size("block")

    def operate(vector_field):
        edges = with_halo(root_stiff[None] * vector_field, (("slab", 1), ("block", 2)), 1)
        padded_weighted = jnp.pad(edges, ((0, 0), (0, 0), (0, 0), (1, 1)))
        return operate_padded(
            vector_field, padded_weighted, padded_root, stiffness, root_stiff, couplings
        )

    def precondition(residual):
        smooth_first = SMOOTH_WEIGHT * residual / diagonal
        remain = residual - operate(smooth_first)
        block_means = jnp.mean(remain, axis=(1, 2, 3))
        gathered = lax.all_gather(block_means, ("slab", "block"), axis=0, tiled=True)
        own_part = jnp.dot(coarse_inverse, gathered, precision=HIGHEST_PRECISION)
        second = smooth_first + own_part[:, None, None, None]
        leftover = residual - operate(second)
        return second + SMOOTH_WEIGHT * leftover / diagonal

    def paired_sums(residual, smoothed, mapped):
        return lax.psum(
            (jnp.sum(residual * smoothed), jnp.sum(mapped * smoothed)), ("slab", "block")
        )

    solution = jnp.zeros_like(lanczos_vector)
    residual = lanczos_vector
    smoothed = precondition(residual)
    mapped = operate(smoothed)
    gamma_now, delta_now = paired_sums(residual, smoothed, mapped)
    step_size = gamma_now / delta_now
    direction = smoothed
    mapped_dir = mapped
    for number in range(ITERS):
        solution = solution + step_size * direction
        residual = residual - step_size * mapped_dir
        if number + 1 < ITERS:
            smoothed = precondition(residual)
            mapped = operate(smoothed)
            gamma_next, delta_now = paired_sums(residual, smoothed, mapped)
            ratio = gamma_next / gamma_now
            step_size = gamma_next / (delta_now - ratio * gamma_next / step_size)
            direction = smoothed + ratio * direction
            mapped_dir = mapped + ratio * mapped_dir
            gamma_now = gamma_next
    inner_part, weight = lax.psum(
        (jnp.sum(lanczos_vector * solution), jnp.sum(lanczos_vector * lanczos_vector)),
        ("slab", "block"),
    )
    alpha_now = inner_part / weight
    lanczos_part = solution - alpha_now * lanczos_vector - previous_beta * previous_vector
    local_proj = jnp.einsum(
        "kcxyz,cxyz->k", locked_vectors, lanczos_part, precision=HIGHEST_PRECISION
    )
    projections = lax.psum(local_proj, ("slab", "block"))
    remainder = lanczos_part - jnp.einsum(
        "kcxyz,k->cxyz", locked_vectors, projections, precision=HIGHEST_PRECISION
    )
    square = lax.psum(jnp.sum(remainder * remainder), ("slab", "block"))
    cell_count = 3.0 * span_x * span_y * span_z * slab_count * block_count
    beta_norm = jnp.sqrt(square / cell_count)
    return (remainder, jnp.stack([alpha_now, beta_norm]), projections)


def solution(mesh):
    in_specs = (
        P(None, "slab", "block", None),
        P(None, "slab", "block", None),
        P(),
        P(None, None, "slab", "block", None),
        P("slab", "block", None),
        P("slab", "block", None),
        P(),
        P(("slab", "block"), None),
    )
    out_specs = (P(None, "slab", "block", None), P(), P())
    return jax.shard_map(shards, mesh=mesh, in_specs=in_specs, out_specs=out_specs, check_vma=False)
```

profile of v0, /device:TPU:0, one launch (start us, length us, event | category | flops | bytes accessed | tf_op | source)
XLA Modules:
  0.0 647.6 jit_solution(7884673104356321382)
XLA Ops:
  3.8 5.5 collective-permute-start
  31.5 3.0 collective-permute-start.2
  36.1 2.3 broadcast_multiply_fusion.8
  39.7 5.5 collective-permute-start.4
  48.6 3.6 collective-permute-start.6
  53.3 1.6 select_maximum_fusion.32
  60.1 1.9 subtract_reduce_fusion.2
  63.8 45.5 %all-reduce.10 = f32[96]{0:T(128)} all-reduce(f32[96]{0:T(128)} %multiply_dynamic-update-slice_fusion.2), channel_id=1, replica_groups=mesh['slab'=4,'block'=8] {'slab','block'}, use_global_device_ids=true, to_apply=%add.10 | all-reduce | flops 96 | bytes 768
  111.6 4.8 collective-permute-start.8
  116.4 1.5 collective-permute-done.8
  119.3 1.5 collective-permute-start.11
  120.8 3.3 collective-permute-done.11
  129.1 1.5 broadcast_multiply_fusion.6
  132.1 5.4 collective-permute-start.12
  137.6 1.5 collective-permute-done.12
  140.4 4.3 collective-permute-start.14
  147.7 3.2 multiply_reduce_fusion.7
  150.9 45.5 %all-reduce.16 = (f32[]{:T(128)}, f32[]{:T(128)}) all-reduce(f32[]{:T(128)} %get-tuple-element.8, f32[]{:T(128)} %get-tuple-element.7), channel_id=1, replica_groups=mesh['slab'=4,'block'=8] {'slab','block'}, use_global_device_ids=true, to_apply=%region_2.3 | all-reduce | flops 2 | bytes 16 | tf_op jit(solution)/shard_map/psum | solution.py:125
  200.5 4.8 collective-permute-start.16
  205.3 1.5 collective-permute-done.16
  208.1 3.4 collective-permute-start.18
  216.6 1.9 subtract_reduce_fusion.1
  220.2 42.9 %all-reduce.11 = f32[96]{0:T(128)} all-reduce(f32[96]{0:T(128)} %multiply_dynamic-update-slice_fusion.1), channel_id=1, replica_groups=mesh['slab'=4,'block'=8] {'slab','block'}, use_global_device_ids=true, to_apply=%add.11 | all-reduce | flops 96 | bytes 768
  265.5 4.8 collective-permute-start.20
  274.5 3.5 collective-permute-done.23
  283.0 1.5 broadcast_multiply_fusion.3
  286.1 5.4 collective-permute-start.24
  294.4 4.5 collective-permute-start.26
  301.7 3.1 multiply_reduce_fusion.5
  304.8 45.5 %all-reduce.15 = (f32[]{:T(128)}, f32[]{:T(128)}) all-reduce(f32[]{:T(128)} %get-tuple-element.6, f32[]{:T(128)} %get-tuple-element.5), channel_id=1, replica_groups=mesh['slab'=4,'block'=8] {'slab','block'}, use_global_device_ids=true, to_apply=%region_7.8 | all-reduce | flops 2 | bytes 16 | tf_op jit(solution)/shard_map/psum | solution.py:125
  357.4 4.8 collective-permute-start.28
  365.0 3.0 collective-permute-start.30
  373.5 1.9 subtract_reduce_fusion
  377.2 43.0 %all-reduce.12 = f32[96]{0:T(128)} all-reduce(f32[96]{0:T(128)} %multiply_dynamic-update-slice_fusion), channel_id=1, replica_groups=mesh['slab'=4,'block'=8] {'slab','block'}, use_global_device_ids=true, to_apply=%add.12 | all-reduce | flops 96 | bytes 768
  422.5 4.8 collective-permute-start.32
  430.2 1.5 collective-permute-start.35
  431.7 3.3 collective-permute-done.35
  440.0 1.5 broadcast_multiply_fusion
  443.1 5.4 collective-permute-start.36
  451.4 4.3 collective-permute-start.38
  458.7 2.2 multiply_reduce_fusion.3
  461.5 45.6 %all-reduce.14 = (f32[]{:T(128)}, f32[]{:T(128)}) all-reduce(f32[]{:T(128)} %multiply_reduce_fusion.4, f32[]{:T(128)} %multiply_reduce_fusion.3), channel_id=1, replica_groups=mesh['slab'=4,'block'=8] {'slab','block'}, use_global_device_ids=true, to_apply=%region_12.13 | all-reduce | flops 2 | bytes 16 | tf_op jit(solution)/shard_map/psum | solution.py:125
  510.9 2.5 multiply_reduce_fusion.1
  513.4 40.2 %all-reduce.13 = (f32[]{:T(128)}, f32[]{:T(128)}) all-reduce(f32[]{:T(128)} %get-tuple-element.4, f32[]{:T(128)} %get-tuple-element.3), channel_id=1, replica_groups=mesh['slab'=4,'block'=8] {'slab','block'}, use_global_device_ids=true, to_apply=%region_16.17 | all-reduce | flops 2 | bytes 16 | tf_op jit(solution)/shard_map/psum | solution.py:149
  556.1 5.0 fusion.4
  561.0 40.5 %psum.78 = f32[16]{0:T(128)S(1)} all-reduce(f32[16]{0:T(128)S(1)} %fusion.4), channel_id=1, replica_groups=mesh['slab'=4,'block'=8] {'slab','block'}, use_global_device_ids=true, to_apply=%region_19.20 | all-reduce | flops 16 | bytes 128 | tf_op jit(solution)/shard_map/psum | solution.py:158
  601.6 3.3 fusion
  606.2 39.7 %psum.79 = f32[]{:T(128)} all-reduce(f32[]{:T(128)} %get-tuple-element.69), channel_id=1, replica_groups=mesh['slab'=4,'block'=8] {'slab','block'}, use_global_device_ids=true, to_apply=%region_21.22 | all-reduce | flops 1 | bytes 8 | tf_op jit(solution)/shard_map/psum | solution.py:162
  (1179 shorter events, 109.2 us)
Async XLA Ops:
  0.6 555.4 %copy-start = (f32[16,3,8,8,256]{4,3,2,1,0:T(8,128)S(1)}, f32[16,3,8,8,256]{4,3,2,1,0:T(8,128)}, u32[]{:S(2)}) copy-start(f32[16,3,8,8,256]{4,3,2,1,0:T(8,128)} %param.11) | copy-start | bytes 9437188
  2.5 27.6 %collective-permute-start.1 = (f32[1,8,256]{2,1,0:T(8,128)S(1)}, f32[1,8,256]{2,1,0:T(8,128)S(1)}, u32[]{:S(2)}, u32[]{:S(2)}) collective-permute-start(f32[1,8,256]{2,1,0:T(8,128)S(1)} %get-tuple-element.1154), channel_id=1, source_target_pairs={{8,0},{16,8},{24,16},{9,1},{17,9},{25,17},{10,2},{18,10},{26,18},{... | collective-permute-start | bytes 24584 | tf_op jit(solution)/shard_map/ppermute | solution.py:24
  3.8 26.3 %collective-permute-start = (f32[1,8,256]{2,1,0:T(8,128)S(1)}, f32[1,8,256]{2,1,0:T(8,128)S(1)}, u32[]{:S(2)}, u32[]{:S(2)}) collective-permute-start(f32[1,8,256]{2,1,0:T(8,128)S(1)} %get-tuple-element.1153), channel_id=1, source_target_pairs={{0,8},{8,16},{16,24},{1,9},{9,17},{17,25},{2,10},{10,18},{18,26},{... | collective-permute-start | bytes 24584 | tf_op jit(solution)/shard_map/ppermute | solution.py:21
  30.2 4.4 collective-permute-start.3
  31.5 3.9 collective-permute-start.2
  35.7 17.3 %copy-start.5 = (f32[8,8,256]{2,1,0:T(8,128)}, f32[8,8,256]{2,1,0:T(8,128)S(1)}, u32[]{:S(2)}) copy-start(f32[8,8,256]{2,1,0:T(8,128)S(1)} %get-tuple-element.360) | copy-start | bytes 196612
  35.8 17.2 %copy-start.12 = (f32[8,8,256]{2,1,0:T(8,128)}, f32[8,8,256]{2,1,0:T(8,128)S(1)}, u32[]{:S(2)}) copy-start(f32[8,8,256]{2,1,0:T(8,128)S(1)} %get-tuple-element.361) | copy-start | bytes 196612
  35.8 17.2 %copy-start.19 = (f32[8,8,256]{2,1,0:T(8,128)}, f32[8,8,256]{2,1,0:T(8,128)S(1)}, u32[]{:S(2)}) copy-start(f32[8,8,256]{2,1,0:T(8,128)S(1)} %get-tuple-element.362) | copy-start | bytes 196612
  38.4 7.6 %collective-permute-start.5 = (f32[3,1,8,256]{3,2,1,0:T(8,128)S(1)}, f32[3,1,8,256]{3,2,1,0:T(8,128)S(1)}, u32[]{:S(2)}, u32[]{:S(2)}) collective-permute-start(f32[3,1,8,256]{3,2,1,0:T(8,128)S(1)} %get-tuple-element.1138), channel_id=1, source_target_pairs={{8,0},{16,8},{24,16},{9,1},{17,9},{25,17},{10,2},{18,10},{26,18},{... | collective-permute-start | bytes 73736 | tf_op jit(solution)/shard_map/ppermute | solution.py:24
  39.7 7.0 %collective-permute-start.4 = (f32[3,1,8,256]{3,2,1,0:T(8,128)S(1)}, f32[3,1,8,256]{3,2,1,0:T(8,128)S(1)}, u32[]{:S(2)}, u32[]{:S(2)}) collective-permute-start(f32[3,1,8,256]{3,2,1,0:T(8,128)S(1)} %get-tuple-element.1137), channel_id=1, source_target_pairs={{0,8},{8,16},{16,24},{1,9},{9,17},{17,25},{2,10},{10,18},{18,26},{... | collective-permute-start | bytes 73736 | tf_op jit(solution)/shard_map/ppermute | solution.py:21
  47.3 6.0 collective-permute-start.7
  48.6 4.7 collective-permute-start.6
  110.3 6.1 collective-permute-start.9
  111.6 6.3 collective-permute-start.8
  118.0 2.8 collective-permute-start.10
  119.3 4.8 collective-permute-start.11
  130.7 6.9 %collective-permute-start.13 = (f32[3,1,8,256]{3,2,1,0:T(8,128)S(1)}, f32[3,1,8,256]{3,2,1,0:T(8,128)S(1)}, u32[]{:S(2)}, u32[]{:S(2)}) collective-permute-start(f32[3,1,8,256]{3,2,1,0:T(8,128)S(1)} %get-tuple-element.973), channel_id=1, source_target_pairs={{8,0},{16,8},{24,16},{9,1},{17,9},{25,17},{10,2},{18,10},{26,18},{... | collective-permute-start | bytes 73736 | tf_op jit(solution)/shard_map/ppermute | solution.py:24
  132.1 7.0 %collective-permute-start.12 = (f32[3,1,8,256]{3,2,1,0:T(8,128)S(1)}, f32[3,1,8,256]{3,2,1,0:T(8,128)S(1)}, u32[]{:S(2)}, u32[]{:S(2)}) collective-permute-start(f32[3,1,8,256]{3,2,1,0:T(8,128)S(1)} %get-tuple-element.972), channel_id=1, source_target_pairs={{0,8},{8,16},{16,24},{1,9},{9,17},{17,25},{2,10},{10,18},{18,26},{... | collective-permute-start | bytes 73736 | tf_op jit(solution)/shard_map/ppermute | solution.py:21
  139.1 5.6 collective-permute-start.15
  140.4 5.1 collective-permute-start.14
  198.9 17.3 %copy-start.160 = (f32[3,8,8,256]{3,2,1,0:T(8,128)}, f32[3,8,8,256]{3,2,1,0:T(8,128)S(1)}, u32[]{:S(2)}) copy-start(f32[3,8,8,256]{3,2,1,0:T(8,128)S(1)} %get-tuple-element.82) | copy-start | bytes 589828
  199.0 6.3 collective-permute-start.17
  200.5 6.3 collective-permute-start.16
  206.8 4.7 collective-permute-start.19
  208.1 3.9 collective-permute-start.18
  264.2 6.1 collective-permute-start.21
  265.5 6.3 collective-permute-start.20
  271.9 2.6 collective-permute-start.22
  273.2 4.9 collective-permute-start.23
  284.7 6.9 %collective-permute-start.25 = (f32[3,1,8,256]{3,2,1,0:T(8,128)S(1)}, f32[3,1,8,256]{3,2,1,0:T(8,128)S(1)}, u32[]{:S(2)}, u32[]{:S(2)}) collective-permute-start(f32[3,1,8,256]{3,2,1,0:T(8,128)S(1)} %get-tuple-element.723), channel_id=1, source_target_pairs={{8,0},{16,8},{24,16},{9,1},{17,9},{25,17},{10,2},{18,10},{26,18},{... | collective-permute-start | bytes 73736 | tf_op jit(solution)/shard_map/ppermute | solution.py:24
  286.1 7.0 %collective-permute-start.24 = (f32[3,1,8,256]{3,2,1,0:T(8,128)S(1)}, f32[3,1,8,256]{3,2,1,0:T(8,128)S(1)}, u32[]{:S(2)}, u32[]{:S(2)}) collective-permute-start(f32[3,1,8,256]{3,2,1,0:T(8,128)S(1)} %get-tuple-element.722), channel_id=1, source_target_pairs={{0,8},{8,16},{16,24},{1,9},{9,17},{17,25},{2,10},{10,18},{18,26},{... | collective-permute-start | bytes 73736 | tf_op jit(solution)/shard_map/ppermute | solution.py:21
  293.1 5.8 collective-permute-start.27
  294.4 5.1 collective-permute-start.26
  355.8 17.3 %copy-start.162 = (f32[3,8,8,256]{3,2,1,0:T(8,128)}, f32[3,8,8,256]{3,2,1,0:T(8,128)S(1)}, u32[]{:S(2)}) copy-start(f32[3,8,8,256]{3,2,1,0:T(8,128)S(1)} %get-tuple-element.76) | copy-start | bytes 589828
  355.9 6.3 collective-permute-start.29
  357.4 6.3 collective-permute-start.28
  363.7 4.3 collective-permute-start.31
  365.0 3.9 collective-permute-start.30
  421.2 6.1 collective-permute-start.33
  422.5 6.3 collective-permute-start.32
  428.9 2.8 collective-permute-start.34
  430.2 4.9 collective-permute-start.35
  441.7 6.9 %collective-permute-start.37 = (f32[3,1,8,256]{3,2,1,0:T(8,128)S(1)}, f32[3,1,8,256]{3,2,1,0:T(8,128)S(1)}, u32[]{:S(2)}, u32[]{:S(2)}) collective-permute-start(f32[3,1,8,256]{3,2,1,0:T(8,128)S(1)} %get-tuple-element.473), channel_id=1, source_target_pairs={{8,0},{16,8},{24,16},{9,1},{17,9},{25,17},{10,2},{18,10},{26,18},{... | collective-permute-start | bytes 73736 | tf_op jit(solution)/shard_map/ppermute | solution.py:24
  443.1 7.0 %collective-permute-start.36 = (f32[3,1,8,256]{3,2,1,0:T(8,128)S(1)}, f32[3,1,8,256]{3,2,1,0:T(8,128)S(1)}, u32[]{:S(2)}, u32[]{:S(2)}) collective-permute-start(f32[3,1,8,256]{3,2,1,0:T(8,128)S(1)} %get-tuple-element.472), channel_id=1, source_target_pairs={{0,8},{8,16},{16,24},{1,9},{9,17},{17,25},{2,10},{10,18},{18,26},{... | collective-permute-start | bytes 73736 | tf_op jit(solution)/shard_map/ppermute | solution.py:21
  450.1 6.3 collective-permute-start.39
  451.4 5.1 collective-permute-start.38
  458.6 52.3 %copy-start.4 = (f32[3,8,8,256]{3,2,1,0:T(8,128)S(1)}, f32[3,8,8,256]{3,2,1,0:T(8,128)}, u32[]{:S(2)}) copy-start(f32[3,8,8,256]{3,2,1,0:T(8,128)} %param.8) | copy-start | bytes 589828
  601.6 45.6 %copy-start.386 = (f32[16]{0:T(128)}, f32[16]{0:T(128)S(1)}, u32[]{:S(2)}) copy-start(f32[16]{0:T(128)S(1)} %psum.78) | copy-start | bytes 196
  (379 other events, 1714.3 us)
where the time goes:
time: 658 us; the launch traced here: 648 us
  blocking collectives  388 us (59%)
  starting transfers between devices  108 us (16%)
  other arithmetic  58.5 us (9%)
  local copies, waits for them, and re-layouts  33.5 us (5%)
  waiting for transfers between devices  26.5 us (4%)
  between operations  21.4 us (3%)
  matrix products  11 us (2%)
    psum x3, blocking collectives, paired_sums(): lax.psum((jnp.sum(residual * smoothed), jnp.sum(mapped * smoothed)), ('sl...  137 us
    unnamed x3, blocking collectives  131 us
    ppermute x20, starting transfers between devices, with_halo(): lax.ppermute(lax.slice_in_dim(block, block.shape[dim] - width, None, axis...  81.4 us
    psum x1, blocking collectives, shards(): projections = lax.psum(local_proj, ('slab', 'block'))  40.5 us
    psum x1, blocking collectives, shards(): lax.psum((jnp.sum(lanczos_vector * solution), jnp.sum(lanczos_vector * la...  40.2 us
    psum x1, blocking collectives, shards(): square = lax.psum(jnp.sum(remainder * remainder), ('slab', 'block'))  39.7 us
    ppermute x20, starting transfers between devices, with_halo(): lax.ppermute(lax.slice_in_dim(block, 0, width, axis=dim), axis, backward)  26.9 us
    ppermute x20, waiting for transfers between devices, with_halo(): lax.ppermute(lax.slice_in_dim(block, block.shape[dim] - width, None, axis...  16.3 us
  transfers between devices with their start and end apart: 40, of which 18 were waited for; matrix products, arithmetic and copies ran while one was open for 4% of the time, Pallas kernels for 0%

commit v1 on v0

v1 whole, which is shorter than its diff:
```python
import functools

import jax
import jax.numpy as jnp
from jax import lax
from jax.experimental import pallas as pl
from jax.experimental.pallas import tpu as pltpu
from jax.sharding import PartitionSpec as P

BRICK = 8
ITERS = 3
SHIFT_MASS = 0.02
SMOOTH_WEIGHT = 0.5
VOID_DENSITY = 0.1

AXES = ("slab", "block")
LANES = 128
WIDE = (8, 24)
MID = (4, 16)
OWN = (0, 8)
REACH = 2 * ITERS
PAIRS = [(n // 9 - 1, n // 3 % 3 - 1, n % 3 - 1) for n in range(13)]
SYM = [(0, 0), (0, 1), (0, 2), (1, 1), (1, 2), (2, 2)]
SLOT = {}
for number, (first, second) in enumerate(SYM):
    SLOT[first, second] = number
    SLOT[second, first] = number

f32 = jnp.float32


def shift_store(dest, at, fields, source, target):
    src_off, src_rows = source
    dst_off, dst_rows = target
    depth = fields[0].shape[1]
    lane = lax.broadcasted_iota(jnp.int32, (dst_rows, depth), 1)
    for comp, field in enumerate(fields):
        for dy in (-1, 0, 1):
            shift = src_off - dst_off + dy
            moved = field if shift == 0 else pltpu.roll(field, (-shift) % src_rows, 0)
            if dst_rows != src_rows:
                moved = moved[:dst_rows]
            for dz in (-1, 0, 1):
                if dz == 0:
                    out = moved
                else:
                    edge = 0 if dz < 0 else depth - 1
                    out = jnp.where(lane == edge, 0.0, pltpu.roll(moved, (-dz) % depth, 1))
                dest[((dy + 1) * 3 + dz + 1) * len(fields) + comp, at] = out


def pair_slots(pair):
    dx, dy, dz = pair
    return dx, (dy + 1) * 3 + dz + 1, (1 - dy) * 3 + 1 - dz


def stencil(moved, at, coup, diag):
    total = [None] * 3
    for number, pair in enumerate(PAIRS):
        dx, plus, minus = pair_slots(pair)
        sums = [moved[plus * 3 + c, at + dx] + moved[minus * 3 + c, at - dx] for c in range(3)]
        for k in range(3):
            for c in range(3):
                term = coup[number * 9 + k * 3 + c] * sums[c]
                total[k] = term if total[k] is None else total[k] + term
    near = [moved[4 * 3 + c, at] for c in range(3)]
    out = []
    for k in range(3):
        acc = diag(SLOT[k, 0]) * near[0] + diag(SLOT[k, 1]) * near[1]
        acc = acc + diag(SLOT[k, 2]) * near[2]
        out.append(acc - total[k])
    return out, near


def loop(low, high, body):
    def step(i, carry):
        body(i)
        return carry

    lax.fori_loop(low, high, step, 0)


def row_sum(x):
    return jnp.sum(x, axis=0, keepdims=True)


def to_lanes(rows):
    column = jnp.sum(rows, axis=1, keepdims=True)
    count = rows.shape[0]
    here = lax.broadcasted_iota(jnp.int32, (count, LANES), 0)
    lane = lax.broadcasted_iota(jnp.int32, (count, LANES), 1)
    return row_sum(jnp.where(here == lane, column, 0.0))


def pick(row, index):
    lane = lax.broadcasted_iota(jnp.int32, row.shape, 1)
    return jnp.sum(jnp.where(lane == index, row, 0.0), axis=1, keepdims=True)


def scalar(one):
    return one[0, 0]


def coarse_values(means, rows_of, where, counts, store):
    total = None
    for k in range(3):
        part = row_sum(rows_of(k) * means[:, k : k + 1])
        total = part if total is None else total + part
    for bx in range(3):
        for by in range(3):
            spot = (where[0] + bx - 1) * counts[1] + where[1] + by - 1
            for k in range(3):
                store[(bx * 3 + by) * 3 + k] = scalar(pick(total, spot * 3 + k))


def correction(store, x, k, layout, span, depth):
    off, rows = layout
    base = lax.div(x + span, span) * 9 + k
    row = lax.broadcasted_iota(jnp.int32, (rows, depth), 0)
    high = jnp.where(row < off + 8, store[base + 3], store[base + 6])
    return jnp.where(row < off, store[base], high)


def send_row(row, count):
    return jnp.broadcast_to(row, (count, row.shape[1]))


def setup_kernel(
    dims, where, coup, even, odd, mid, cinv,
    kh_w, h_w, v_w, root_w, kh_m, h_m, v_m, root_m, msg,
    moved_root, root_all, moved_own, sums,
):
    span, depth, devices = dims
    halo = REACH + 1
    flip = where[1] % 2 == 1

    def wide(comp, x):
        first, second = even[comp, x], odd[comp, x]
        low = jnp.where(flip, first, second)
        high = jnp.where(flip, second, first)
        return jnp.concatenate([low, mid[comp, x], high], axis=0)

    def roots(x):
        root = jnp.sqrt(wide(3, x))
        root_all[x] = root
        shift_store(moved_root, x, [root], WIDE, WIDE)

    loop(0, span + 2 * halo, roots)

    def repack(field):
        return pltpu.roll(field, WIDE[1] - (WIDE[0] - MID[0]), 0)[: MID[1]]

    def diagonals(x, also_mid):
        at = x + 1
        total = [None] * 6
        for number, pair in enumerate(PAIRS):
            dx, plus, minus = pair_slots(pair)
            both = moved_root[plus, at + dx] + moved_root[minus, at - dx]
            for slot, (k, c) in enumerate(SYM):
                term = coup[number * 9 + k * 3 + c] * both
                total[slot] = term if total[slot] is None else total[slot] + term
        root = root_all[at]
        inside = root > 0.0
        inverse = jnp.where(inside, 1.0 / jnp.where(inside, root, 1.0), 0.0)
        root_w[x] = root
        m = x - (REACH - 4)
        if also_mid:
            root_m[m] = repack(root)
        for slot, (k, c) in enumerate(SYM):
            value = total[slot] * inverse
            if k == c:
                value = value + SHIFT_MASS
                half = jnp.where(inside, SMOOTH_WEIGHT / value, 0.0)
                h_w[k, x] = half
                vector = wide(k, at) * inverse
                v_w[k, x] = vector
                if also_mid:
                    h_m[k, m] = repack(half)
                    v_m[k, m] = repack(vector)
            kh_w[slot, x] = value
            if also_mid:
                kh_m[slot, m] = repack(value)

    edge = REACH - 4
    loop(0, edge, lambda x: diagonals(x, False))
    loop(edge, edge + span + 8, lambda x: diagonals(x, True))
    loop(edge + span + 8, span + 2 * REACH, lambda x: diagonals(x, False))

    def smooth(x):
        at = x + REACH - 1
        shift_store(moved_own, x, [h_w[k, at] * v_w[k, at] for k in range(3)], WIDE, OWN)

    loop(0, span + 2, smooth)

    def remain(x, carry):
        at = x + REACH
        own = slice(WIDE[0], WIDE[0] + 8)
        image, _ = stencil(moved_own, x + 1, coup, lambda slot: kh_w[slot, at, own])
        return tuple(carry[k] + root_w[at, own] * (v_w[k, at, own] - image[k]) for k in range(3))

    zero = jnp.zeros((8, depth), f32)
    parts = lax.fori_loop(0, span, remain, (zero, zero, zero))
    sums[...] = jnp.zeros_like(sums)
    for k in range(3):
        sums[k : k + 1] = row_sum(parts[k])
    row = to_lanes(sums[...]) * (1.0 / (span * 8 * depth))
    msg[:, :LANES] = send_row(row, devices)
    width = cinv.shape[1]
    padded = (msg.shape[1] - LANES) // 3
    for k in range(3):
        low = LANES + k * padded
        if padded != width:
            msg[:, low : low + padded] = jnp.zeros((devices, padded), f32)
        msg[:, low : low + width] = jnp.broadcast_to(cinv[k : k + 1], (devices, width))


def iterate(dims, level, layouts, coup, store, residual, half, root, diag, moved, moved_next, own_z):
    span, depth = dims
    source, first, second = layouts

    def begin(x):
        fields = []
        for k in range(3):
            fix = correction(store, x - level, k, source, span, depth)
            fields.append(half(k, x) * residual(k, x) + root(x) * fix)
        shift_store(moved, x, fields, source, first)

    loop(0, span + 2 * level, begin)

    def middle(x):
        at = x + 1
        image, near = stencil(moved, at, coup, diag[0](at))
        fields = [near[k] + half(k, at) * (residual(k, at) - image[k]) for k in range(3)]
        own_z(x, fields)
        shift_store(moved_next, x, fields, first, second)

    loop(0, span + 2 * level - 2, middle)


def own_rows(layout):
    return slice(layout[0], layout[0] + 8)


def means_of(dims, coup, root, half, mapped, diag, moved_own):
    span, depth = dims

    def begin(x):
        shift_store(moved_own, x, [half(k, x) * mapped(k, x) for k in range(3)], MID, OWN)

    loop(0, span + 2, begin)

    def body(x, carry):
        image, _ = stencil(moved_own, x + 1, coup, lambda slot: diag(slot, x))
        return tuple(carry[k] + root(x) * (mapped_own(k, x) - image[k]) for k in range(3))

    def mapped_own(k, x):
        return pltpu.roll(mapped(k, x + 1), MID[1] - MID[0], 0)[:8]

    zero = jnp.zeros((8, depth), f32)
    return lax.fori_loop(0, span, body, (zero, zero, zero))


def own_of(field):
    return pltpu.roll(field, MID[1] - MID[0], 0)[:8]


def first_kernel(
    dims, counts, where, coup, got, kh_w, h_w, v_w, root_w, kh_m, h_m,
    z_own, mapped, msg,
    moved, moved_next, moved_own, store, sums,
):
    span, depth, devices = dims
    level = REACH
    padded = (got.shape[1] - LANES) // 3
    coarse_values(
        got[:, :LANES],
        lambda k: got[:, LANES + k * padded : LANES + (k + 1) * padded],
        where, counts, store,
    )

    def keep(x, fields):
        at = x - (level - 1)

        @pl.when((at >= 0) & (at < span))
        def _():
            for k in range(3):
                z_own[k, at] = fields[k][own_rows(WIDE)]

    iterate(
        (span, depth), level, (WIDE, WIDE, MID), coup, store,
        lambda k, x: v_w[k, x], lambda k, x: h_w[k, x], lambda x: root_w[x],
        (lambda at: lambda slot: kh_w[slot, at],), moved, moved_next, keep,
    )

    def image(x):
        out, _ = stencil(moved_next, x + 1, coup, lambda slot: kh_m[slot, x])
        for k in range(3):
            mapped[k, x] = out[k]

    loop(0, span + 2 * level - 4, image)
    inner = level - 2
    parts = means_of(
        (span, depth), coup,
        lambda x: root_w[x + REACH, own_rows(WIDE)],
        lambda k, x: h_m[k, x + 3], lambda k, x: mapped[k, x + inner - 1],
        lambda slot, x: kh_w[slot, x + REACH, own_rows(WIDE)], moved_own,
    )

    def dots(x, carry):
        gamma, delta = carry
        for k in range(3):
            z = z_own[k, x]
            gamma = gamma + v_w[k, x + REACH, own_rows(WIDE)] * z
            delta = delta + own_of(mapped[k, x + inner]) * z
        return gamma, delta

    zero = jnp.zeros((8, depth), f32)
    gamma, delta = lax.fori_loop(0, span, dots, (zero, zero))
    scale = 1.0 / (span * 8 * depth)
    sums[...] = jnp.zeros_like(sums)
    for k in range(3):
        sums[k : k + 1] = row_sum(parts[k]) * scale
    sums[3:4] = row_sum(gamma)
    sums[4:5] = row_sum(delta)
    msg[...] = send_row(to_lanes(sums[...]), devices)


def second_kernel(
    dims, counts, where, coup, got, first, kh_m, h_m, v_m, root_m, kh_w, z_old, mapped_old,
    z_own, mapped, residual, means, msg,
    moved, moved_next, moved_own, store, sums,
):
    span, depth, devices = dims
    level = REACH - 2
    total = row_sum(got[...])
    gamma = pick(total, 3)
    step = gamma / pick(total, 4)
    padded = (first.shape[1] - LANES) // 3
    means[...] = first[:, :LANES] - step * got[...]
    coarse_values(
        means[...],
        lambda k: first[:, LANES + k * padded : LANES + (k + 1) * padded],
        where, counts, store,
    )
    size = scalar(step)

    def update(x):
        for k in range(3):
            residual[k, x] = v_m[k, x] - size * mapped_old[k, x]

    loop(0, span + 2 * level, update)

    def keep(x, fields):
        at = x - (level - 1)

        @pl.when((at >= 0) & (at < span))
        def _():
            for k in range(3):
                z_own[k, at] = own_of(fields[k])

    iterate(
        (span, depth), level, (MID, MID, MID), coup, store,
        lambda k, x: residual[k, x], lambda k, x: h_m[k, x], lambda x: root_m[x],
        (lambda at: lambda slot: kh_m[slot, at],), moved, moved_next, keep,
    )

    def image(x):
        out, _ = stencil(moved_next, x + 1, coup, lambda slot: kh_m[slot, x + 2])
        for k in range(3):
            mapped[k, x] = out[k]

    loop(0, span + 2 * level - 4, image)
    inner = level - 2
    parts = means_of(
        (span, depth), coup,
        lambda x: own_of(root_m[x + 4]),
        lambda k, x: h_m[k, x + 3], lambda k, x: mapped[k, x + inner - 1],
        lambda slot, x: kh_w[slot, x + REACH, own_rows(WIDE)], moved_own,
    )

    def dots(x, carry):
        gamma, delta, cross = carry
        for k in range(3):
            z = z_own[k, x]
            gamma = gamma + own_of(residual[k, x + level]) * z
            delta = delta + own_of(mapped[k, x + inner]) * z
            cross = cross + own_of(mapped_old[k, x + 4]) * z
        return gamma, delta, cross

    zero = jnp.zeros((8, depth), f32)
    dotted = lax.fori_loop(0, span, dots, (zero, zero, zero))
    scale = 1.0 / (span * 8 * depth)
    sums[...] = jnp.zeros_like(sums)
    for k in range(3):
        sums[k : k + 1] = row_sum(parts[k]) * scale
        sums[k + 3 : k + 4] = row_sum(dotted[k])
    msg[...] = send_row(to_lanes(sums[...]), devices)


def third_kernel(
    dims, counts, where, coup, beta, got, got_old, first, means, kh_m, h_m, root_m, kh_w, v_w, root_w,
    z_old, mapped_old, z_new, mapped_new, residual_old, lanczos, previous, locked,
    base, z_out, dir_out, scal, msg,
    moved, moved_next, residual, mapped, store, sums, locked_sums,
):
    span, depth, devices = dims
    level = REACH - 4
    total_old = row_sum(got_old[...])
    total = row_sum(got[...])
    gamma_old = pick(total_old, 3)
    delta_old = pick(total_old, 4)
    step_old = gamma_old / delta_old
    gamma = pick(total, 3)
    ratio = gamma / gamma_old
    delta = pick(total, 4) + 2.0 * ratio * pick(total, 5) + ratio * ratio * delta_old
    step = gamma / delta
    fresh = means[...] - step * (got[...] + ratio * got_old[...])
    padded = (first.shape[1] - LANES) // 3
    coarse_values(
        fresh,
        lambda k: first[:, LANES + k * padded : LANES + (k + 1) * padded],
        where, counts, store,
    )
    lane = lax.broadcasted_iota(jnp.int32, (1, LANES), 1)
    scal[...] = jnp.where(lane == 0, gamma, jnp.where(lane == 1, delta, 0.0))
    size, size_old, blend = scalar(step), scalar(step_old), scalar(ratio)

    def update(x):
        for k in range(3):
            mapped[k, x] = mapped_new[k, x] + blend * mapped_old[k, x + 2]
            residual[k, x] = residual_old[k, x + 2] - size * mapped[k, x]

    loop(0, span + 2 * level, update)

    def keep(x, fields):
        at = x - (level - 1)

        @pl.when((at >= 0) & (at < span))
        def _():
            for k in range(3):
                z_out[k, at] = own_of(fields[k])

    iterate(
        (span, depth), level, (MID, MID, OWN), coup, store,
        lambda k, x: residual[k, x], lambda k, x: h_m[k, x + 2], lambda x: root_m[x + 2],
        (lambda at: lambda slot: kh_m[slot, at + 2],), moved, moved_next, keep,
    )

    def finish(x, carry):
        gamma, delta, cross, with_base, with_z, with_dir, weight = carry
        own = own_rows(WIDE)
        image, _ = stencil(moved_next, x + 1, coup, lambda slot: kh_w[slot, x + REACH, own])
        inverse = 1.0 / root_w[x + REACH, own]
        for k in range(3):
            z = z_out[k, x]
            direction = z_new[k, x] + blend * z_old[k, x]
            partial = size_old * z_old[k, x] + size * direction
            vector = v_w[k, x + REACH, own]
            gamma = gamma + own_of(residual[k, x + level]) * z
            delta = delta + image[k] * z
            cross = cross + own_of(mapped[k, x + level]) * z
            with_base = with_base + vector * partial
            with_z = with_z + vector * z
            with_dir = with_dir + vector * direction
            weight = weight + lanczos[k, x] * lanczos[k, x]
            z_out[k, x] = z * inverse
            dir_out[k, x] = direction * inverse
            base[k, x] = partial * inverse - beta[0] * previous[k, x]
        return gamma, delta, cross, with_base, with_z, with_dir, weight

    zero = jnp.zeros((8, depth), f32)
    dotted = lax.fori_loop(0, span, finish, (zero,) * 7)
    sums[...] = jnp.zeros_like(sums)
    for k in range(7):
        sums[k : k + 1] = row_sum(dotted[k])

    def project(n):
        def body(x, carry):
            out = list(carry)
            for k in range(3):
                vector = locked[n, k, x]
                out[0] = out[0] + vector * base[k, x]
                out[1] = out[1] + vector * z_out[k, x]
                out[2] = out[2] + vector * dir_out[k, x]
                out[3] = out[3] + vector * lanczos[k, x]
            return tuple(out)

        four = lax.fori_loop(0, span, body, (zero,) * 4, unroll=True)
        rows = [row_sum(one) for one in four]
        locked_sums[n] = jnp.concatenate(rows, axis=0)

    count = locked.shape[0]
    loop(0, count, project)
    msg[:, :LANES] = send_row(to_lanes(sums[...]), devices)
    flat = locked_sums[...].reshape(count * 4, depth)
    msg[:, LANES:] = send_row(to_lanes(flat), devices)


def last_kernel(
    dims, got, scal, base, z, direction, lanczos, locked,
    remainder, out, msg,
    weights, sums,
):
    span, depth, devices = dims
    count = locked.shape[0]
    total = row_sum(got[...])
    head, tail = total[:, :LANES], total[:, LANES:]
    gamma_old, delta_old = pick(scal[...], 0), pick(scal[...], 1)
    gamma = pick(head, 0)
    ratio = gamma / gamma_old
    delta = pick(head, 1) + 2.0 * ratio * pick(head, 2) + ratio * ratio * delta_old
    step = gamma / delta
    inner = pick(head, 3) + step * (pick(head, 4) + ratio * pick(head, 5))
    alpha = inner / pick(head, 6)
    lane = lax.broadcasted_iota(jnp.int32, (1, LANES), 1)
    kind = lane % 4
    factor = jnp.where(kind == 0, 1.0, jnp.where(kind == 1, step, jnp.where(kind == 2, step * ratio, -alpha)))
    terms = jnp.where(lane < 4 * count, tail * factor, 0.0)
    row = jnp.where(lane == count, alpha, 0.0)
    for n in range(count):
        value = jnp.sum(jnp.where(lane // 4 == n, terms, 0.0), axis=1, keepdims=True)
        row = jnp.where(lane == n, value, row)
        weights[n] = scalar(value)
    out[...] = row
    size, both, shrink = scalar(step), scalar(step * ratio), scalar(alpha)

    def body(x, square):
        for k in range(3):
            rest = base[k, x] + size * z[k, x] + both * direction[k, x] - shrink * lanczos[k, x]
            taken = weights[0] * locked[0, k, x]
            for n in range(1, count):
                taken = taken + weights[n] * locked[n, k, x]
            rest = rest - taken
            remainder[k, x] = rest
            square = square + rest * rest
        return square

    square = lax.fori_loop(0, span, body, jnp.zeros((8, depth), f32))
    sums[...] = jnp.zeros_like(sums)
    sums[0:1] = row_sum(square)
    msg[...] = send_row(to_lanes(sums[...]), devices)


VMEM = pl.BlockSpec(memory_space=pltpu.VMEM)
SMEM = pl.BlockSpec(memory_space=pltpu.SMEM)


def call(kernel, name, outs, scratch, smem, *operands, limit=60 << 20):
    return pl.pallas_call(
        kernel,
        name=name,
        out_shape=[jax.ShapeDtypeStruct(shape, f32) for shape in outs],
        in_specs=[SMEM] * smem + [VMEM] * (len(operands) - smem),
        out_specs=[VMEM] * len(outs),
        scratch_shapes=scratch,
        compiler_params=pltpu.CompilerParams(vmem_limit_bytes=limit),
    )(*operands)


def swap_permutes(axis):
    count = lax.axis_size(axis)
    near = [(i, i ^ 1) for i in range(count) if i ^ 1 < count]
    far = [(i, ((i + 1) ^ 1) - 1) for i in range(count)]
    return near, [(i, j) for i, j in far if 0 <= j < count]


def exchange_rows(rows):
    return lax.all_to_all(rows, AXES, 0, 0, tiled=True)


def shards(
    lanczos_vector, previous_vector, previous_beta, locked_vectors, occupancy, young, couplings, coarse_inverse
):
    _, span, span_y, depth = lanczos_vector.shape
    counts = (lax.axis_size("slab"), lax.axis_size("block"))
    devices = counts[0] * counts[1]
    locked = locked_vectors.shape[0]
    halo = REACH + 1
    assert span_y == 8 and span >= halo and locked * 4 <= LANES
    slab, block = lax.axis_index("slab"), lax.axis_index("block")
    where = jnp.stack([slab, block]).astype(jnp.int32)
    coup = couplings.reshape(-1)

    density = jnp.where(occupancy == 1, 1.0, VOID_DENSITY).astype(f32)
    density = jnp.repeat(jnp.repeat(jnp.repeat(density, BRICK, 0), BRICK, 1), BRICK, 2)
    stiffness = density * young
    fields = jnp.concatenate([lanczos_vector, stiffness[None]], axis=0)

    odd = slab % 2
    near, far = swap_permutes("slab")
    upper = lax.slice_in_dim(fields, span - halo, span, axis=1)
    lower = lax.slice_in_dim(fields, 0, halo, axis=1)
    from_near = lax.ppermute(jnp.where(odd == 0, upper, lower), "slab", near)
    from_far = lax.ppermute(jnp.where(odd == 0, lower, upper), "slab", far)
    below = jnp.where(odd == 0, from_far, from_near)
    above = jnp.where(odd == 0, from_near, from_far)
    tall = jnp.concatenate([below, fields, above], axis=1)
    near, far = swap_permutes("block")
    side_near = lax.ppermute(tall, "block", near)
    side_far = lax.ppermute(tall, "block", far)

    dims = (span, depth, devices)
    wide = (span + 2 * REACH, WIDE[1], depth)
    mid = (span + 8, MID[1], depth)
    padded = -(-coarse_inverse.shape[1] // LANES) * LANES

    def scratch(*shape):
        return pltpu.VMEM(shape, f32)

    kh_w, h_w, v_w, root_w, kh_m, h_m, v_m, root_m, msg = call(
        functools.partial(setup_kernel, dims),
        "setup",
        [(6, *wide), (3, *wide), (3, *wide), wide, (6, *mid), (3, *mid), (3, *mid), mid, (devices, LANES + 3 * padded)],
        [
            scratch(9, span + 2 * halo, WIDE[1], depth),
            scratch(span + 2 * halo, WIDE[1], depth),
            scratch(27, span + 2, 8, depth),
            scratch(8, depth),
        ],
        2,
        where, coup, side_near, side_far, tall, coarse_inverse,
    )
    first = exchange_rows(msg)

    own = (3, span, 8, depth)
    store = pltpu.SMEM((27,), f32)
    z_0, mapped_0, msg = call(
        functools.partial(first_kernel, dims, counts),
        "first",
        [own, (3, *mid), (devices, LANES)],
        [
            scratch(27, *wide),
            scratch(27, span + 2 * REACH - 2, MID[1], depth),
            scratch(27, span + 2, 8, depth),
            store,
            scratch(8, depth),
        ],
        2,
        where, coup, first, kh_w, h_w, v_w, root_w, kh_m, h_m,
    )
    got_0 = exchange_rows(msg)

    level = REACH - 2
    inner = (3, span + 2 * level - 4, MID[1], depth)
    z_1, mapped_1, residual, means, msg = call(
        functools.partial(second_kernel, dims, counts),
        "second",
        [own, inner, (3, *mid), (devices, LANES), (devices, LANES)],
        [
            scratch(27, *mid),
            scratch(27, span + 2 * level - 2, MID[1], depth),
            scratch(27, span + 2, 8, depth),
            store,
            scratch(8, depth),
        ],
        2,
        where, coup, got_0, first, kh_m, h_m, v_m, root_m, kh_w, z_0, mapped_0,
    )
    got_1 = exchange_rows(msg)

    level = REACH - 4
    base, z_2, direction, scal, msg = call(
        functools.partial(third_kernel, dims, counts),
        "third",
        [own, own, own, (1, LANES), (devices, 2 * LANES)],
        [
            scratch(27, span + 2 * level, MID[1], depth),
            scratch(27, span + 2 * level - 2, 8, depth),
            scratch(3, span + 2 * level, MID[1], depth),
            scratch(3, span + 2 * level, MID[1], depth),
            store,
            scratch(8, depth),
            scratch(locked, 4, depth),
        ],
        3,
        where, coup, previous_beta.reshape(1), got_1, got_0, first, means, kh_m, h_m, root_m, kh_w, v_w, root_w,
        z_0, mapped_0, z_1, mapped_1, residual, lanczos_vector, previous_vector, locked_vectors,
    )
    got_2 = exchange_rows(msg)

    remainder, row, msg = call(
        functools.partial(last_kernel, dims),
        "last",
        [own, (1, LANES), (devices, LANES)],
        [pltpu.SMEM((locked,), f32), scratch(8, depth)],
        0,
        got_2, scal, base, z_2, direction, lanczos_vector, locked_vectors,
    )
    square = jnp.sum(exchange_rows(msg)[:, 0])
    cell_count = 3.0 * span * span_y * depth * devices
    beta_norm = jnp.sqrt(square / cell_count)
    return remainder, jnp.stack([row[0, locked], beta_norm]), row[0, :locked]


def solution(mesh):
    in_specs = (
        P(None, "slab", "block", None),
        P(None, "slab", "block", None),
        P(),
        P(None, None, "slab", "block", None),
        P("slab", "block", None),
        P("slab", "block", None),
        P(),
        P(("slab", "block"), None),
    )
    out_specs = (P(None, "slab", "block", None), P(), P())
    return jax.shard_map(shards, mesh=mesh, in_specs=in_specs, out_specs=out_specs, check_vma=False)
```

time: 658 us -> 160 us (0.24); the launches traced: 648 us -> 160 us
  blocking collectives: 388 us -> 40.7 us
  starting transfers between devices: 108 us -> 12.2 us
  Pallas kernels: 0 us -> 69.4 us
  other arithmetic: 58.5 us -> 5.29 us
  local copies, waits for them, and re-layouts: 33.5 us -> 8.6 us
  between operations: 21.4 us -> 2.11 us
  matrix products: 11 us -> 0 us
    psum x6 -> x0, blocking collectives: 257 us -> none  [the longest x3 137 us: paired_sums(): lax.psum((jnp.sum(residual * smoothed), jnp.sum(mapped * smoothed)), ('sl...]
    unnamed x3 -> x0, blocking collectives: 131 us -> none
    ppermute x40 -> x4, starting transfers between devices: 108 us -> 7.21 us  [the longest x1 5.76 us: shards(): from_near = lax.ppermute(jnp.where(odd == 0, upper, lower), 'slab', near)]
    pallas_call x0 -> x5, Pallas kernels: none -> 69.4 us  [call(): pl.pallas_call(kernel, name=name, out_shape=[jax.ShapeDtypeStruct(shape,...]
    all_to_all x0 -> x3, blocking collectives: none -> 40.7 us  [exchange_rows(): return lax.all_to_all(rows, AXES, 0, 0, tiled=True)]
    reduce_sum x9 -> x1, other arithmetic: 18.6 us -> 0.6 us  [shards(): square = jnp.sum(exchange_rows(msg)[:, 0])]
    ppermute x40 -> x4, waiting for transfers between devices: 26.5 us -> 10.2 us  [the longest x1 10.1 us: shards(): from_near = lax.ppermute(jnp.where(odd == 0, upper, lower), 'slab', near)]
    sub x31 -> x0, other arithmetic: 15.9 us -> none  [the longest x30 14.9 us: operate_padded(): differ = root_near[None] * vector_field - weighted_near]
  transfers between devices with their start and end apart: 40 -> 6, of which waited for: 18 -> 4; matrix products, arithmetic and copies ran while one was open for 4% -> 2% of each run, Pallas kernels for 0% -> 0%
where the time goes in v1:
time: 160 us
  Pallas kernels  69.4 us (43%)
  blocking collectives  40.7 us (25%)
  waiting for transfers between devices  21.5 us (13%)
  starting transfers between devices  12.2 us (8%)
  local copies, waits for them, and re-layouts  8.6 us (5%)
  other arithmetic  5.29 us (3%)
  between operations  2.11 us (1%)
    pallas_call x5, Pallas kernels, call(): pl.pallas_call(kernel, name=name, out_shape=[jax.ShapeDtypeStruct(shape,...  69.4 us
    all_to_all x3, blocking collectives, exchange_rows(): return lax.all_to_all(rows, AXES, 0, 0, tiled=True)  40.7 us
    all_to_all x2, waiting for transfers between devices, exchange_rows(): return lax.all_to_all(rows, AXES, 0, 0, tiled=True)  11.3 us
    ppermute x1, waiting for transfers between devices, shards(): from_near = lax.ppermute(jnp.where(odd == 0, upper, lower), 'slab', near)  10.1 us
    ppermute x1, starting transfers between devices, shards(): from_near = lax.ppermute(jnp.where(odd == 0, upper, lower), 'slab', near)  5.76 us
    all_to_all x2, starting transfers between devices, exchange_rows(): return lax.all_to_all(rows, AXES, 0, 0, tiled=True)  5 us
    unnamed x15, local copies, waits for them, and re-layouts  3.72 us
  transfers between devices with their start and end apart: 6, of which 4 were waited for; matrix products, arithmetic and copies ran while one was open for 2% of the time, Pallas kernels for 0%

profile of v1, /device:TPU:0, one launch (start us, length us, event | category | flops | bytes accessed | tf_op | source)
XLA Modules:
  0.0 159.8 jit_solution(10528160247842664680)
XLA Ops:
  0.6 0.0 copy-start
  0.7 0.7 fusion.3
  1.4 0.1 broadcast_in_dim.22
  1.4 0.1 broadcast_in_dim.23
  1.5 0.8 multiply_bitcast_fusion
  2.4 0.0 copy-start.5
  2.4 1.1 fusion.1
  3.5 0.7 collective-permute-start
  4.2 5.8 %collective-permute-start.1 = (f32[4,7,8,256]{3,2,1,0:T(8,128)S(1)}, f32[4,7,8,256]{3,2,1,0:T(8,128)S(1)}, u32[]{:S(2)}, u32[]{:S(2)}) collective-permute-start(f32[4,7,8,256]{3,2,1,0:T(8,128)S(1)} %get-tuple-element.56), channel_id=1, source_target_pairs={{0,8},{8,0},{16,24},{24,16},{1,9},{9,1},{17,25},{25,17},{2,10},{10... | collective-permute-start | bytes 688136 | tf_op jit(solution)/shard_map/ppermute | solution.py:593
  9.9 0.0 collective-permute-done
  10.0 10.1 %collective-permute-done.1 = f32[4,7,8,256]{3,2,1,0:T(8,128)S(1)} collective-permute-done((f32[4,7,8,256]{3,2,1,0:T(8,128)S(1)}, f32[4,7,8,256]{3,2,1,0:T(8,128)S(1)}, u32[]{:S(2)}, u32[]{:S(2)}) %collective-permute-start.1) | collective-permute-done | bytes 229408 | tf_op jit(solution)/shard_map/ppermute | solution.py:593
  20.1 0.0 copy-done
  20.1 0.1 pad_maximum_fusion.mid
  20.2 0.0 copy-start.1
  20.2 0.1 collective-permute-start.2
  20.3 0.7 collective-permute-start.3
  21.0 0.0 copy-done.5
  21.0 0.1 copy.13
  21.1 0.6 reshape.27.coup
  21.8 0.6 pad_add_fusion.where
  22.4 0.1 collective-permute-done.2.even
  22.5 0.0 copy-start.2
  22.5 0.0 collective-permute-done.3.odd
  22.5 0.0 copy-done.1
  22.5 0.9 copy-done.2
  23.4 0.0 copy-start.3
  23.4 0.9 copy-done.3
  24.2 13.7 %setup.1 = (f32[6,20,24,256]{3,2,1,0:T(8,128)}, f32[3,20,24,256]{3,2,1,0:T(8,128)}, f32[3,20,24,256]{3,2,1,0:T(8,128)}, f32[20,24,256]{2,1,0:T(8,128)}, f32[6,16...) custom-call(s32[2]{0:T(128)} %pad_add_fusion.where, ...), custom_call_target="tpu_custom_call" | custom-call | tf_op jit(solution)/shard_map/setup/pallas_call | solution.py:549
  37.9 0.9 copy.14
  38.8 21.6 %all_to_all.56 = f32[32,1,512]{2,1,0:T(1,128)S(1)} all-to-all(f32[32,1,512]{2,1,0:T(1,128)S(1)} %copy.14), channel_id=1, replica_groups=mesh['slab'=4,'block'=8] {'slab','block'}, dimensions={0} | all-to-all | bytes 131072 | tf_op jit(solution)/shard_map/all_to_all | solution.py:568
  60.4 0.6 copy.23
  61.0 21.6 %first.1 = (f32[3,8,8,256]{3,2,1,0:T(8,128)}, f32[3,16,16,256]{3,2,1,0:T(8,128)}, f32[32,128]{1,0:T(8,128)}) custom-call(s32[2]{0:T(128)} %pad_add_fusion.where, f32[117]{0:T(128)} %reshape.27.coup, f32[32,512]{1,0:T(8,128)} %bitcast.32, f32[6,20,24,256]{3,2,1,0:T(8,128)} %get-tuple-element.29.kh_w, f32[3,20,24,256]{3,2,1,0:T(8,128)} %get-tuple-element.30.h_w, ...), custom_call_target="tpu_custom_call" | custom-call | tf_op jit(solution)/shard_map/first/pallas_call | solution.py:549
  82.6 10.2 %all_to_all.57 = f32[32,1,128]{2,1,0:T(1,128)} all-to-all(f32[32,1,128]{2,1,0:T(1,128)} %bitcast.44), channel_id=1, replica_groups=mesh['slab'=4,'block'=8] {'slab','block'}, dimensions={0} | all-to-all | bytes 32768 | tf_op jit(solution)/shard_map/all_to_all | solution.py:568
  92.8 16.7 %second.1 = (f32[3,8,8,256]{3,2,1,0:T(8,128)}, f32[3,12,16,256]{3,2,1,0:T(8,128)}, f32[3,16,16,256]{3,2,1,0:T(8,128)}, f32[32,128]{1,0:T(8,128)}, f32[32,128]{1,0:T(8,128)}) custom-call(s32[2]{0:T(128)} %pad_add_fusion.where, f32[117]{0:T(128)} %reshape.27.coup, f32[32,128]{1,0:T(8,128)} %bitcast.35, f32[32,512]{1,0:T(8,128)} %bitcast.33, ...), custom_call_target="tpu_custom_call" | custom-call | tf_op jit(solution)/shard_map/second/pallas_call | solution.py:549
  109.5 2.5 %all-to-all-start.2 = ((f32[32,1,128]{2,1,0:T(1,128)}), f32[32,1,128]{2,1,0:T(1,128)S(1)}, u32[]{:S(2)}, u32[]{:S(2)}) async-start(f32[32,1,128]{2,1,0:T(1,128)} %bitcast.43), calls=%async_computation.2 | async-start | bytes 32768 | tf_op jit(solution)/shard_map/all_to_all | solution.py:568
  112.6 6.5 %all-to-all-done.2 = f32[32,1,128]{2,1,0:T(1,128)S(1)} async-done(((f32[32,1,128]{2,1,0:T(1,128)}), f32[32,1,128]{2,1,0:T(1,128)S(1)}, u32[]{:S(2)}, u32[]{:S(2)}) %all-to-all-start.2) | async-done | bytes 16416 | tf_op jit(solution)/shard_map/all_to_all | solution.py:568
  119.2 0.6 copy-done.4
  119.8 13.8 %third.1 = (f32[3,8,8,256]{3,2,1,0:T(8,128)}, f32[3,8,8,256]{3,2,1,0:T(8,128)}, f32[3,8,8,256]{3,2,1,0:T(8,128)}, f32[1,128]{1,0:T(1,128)}, f32[32,256]{1,0:T(8,128)}) custom-call(s32[2]{0:T(128)} %pad_add_fusion.where, f32[117]{0:T(128)} %reshape.27.coup, f32[1]{0:T(128)} %bitcast.31.beta, f32[32,128]{1,0:T(8,128)} %bitcast.38, f32[32,128]{1,0:T(8,128)} %bitcast.36, ...), custom_call_target="tpu_custom_call" | custom-call | tf_op jit(solution)/shard_map/third/pallas_call | solution.py:549
  133.6 0.8 copy.17
  134.4 8.9 %all_to_all.58 = f32[32,1,256]{2,1,0:T(1,128)S(1)} all-to-all(f32[32,1,256]{2,1,0:T(1,128)S(1)} %copy.17), channel_id=1, replica_groups=mesh['slab'=4,'block'=8] {'slab','block'}, dimensions={0} | all-to-all | bytes 65536 | tf_op jit(solution)/shard_map/all_to_all | solution.py:568
  143.4 0.6 copy.24
  144.0 3.6 %last.1 = (f32[3,8,8,256]{3,2,1,0:T(8,128)}, f32[1,128]{1,0:T(1,128)}, f32[32,128]{1,0:T(8,128)}) custom-call(f32[32,256]{1,0:T(8,128)} %bitcast.37, f32[1,128]{1,0:T(1,128)} %get-tuple-element.46.scal, f32[3,8,8,256]{3,2,1,0:T(8,128)} %get-tuple-element.47.base, f32[3,8,8,256]{3,2,1,0:T(8,128)} %get-tuple-element.48.z, ...), custom_call_target="tpu_custom_call" | custom-call | tf_op jit(solution)/shard_map/last/pallas_call | solution.py:549
  147.6 2.5 %all-to-all-start.4 = ((f32[32,1,128]{2,1,0:T(1,128)}), f32[32,1,128]{2,1,0:T(1,128)S(1)}, u32[]{:S(2)}, u32[]{:S(2)}) async-start(f32[32,1,128]{2,1,0:T(1,128)} %bitcast.42), calls=%async_computation.4 | async-start | bytes 32768 | tf_op jit(solution)/shard_map/all_to_all | solution.py:568
  150.1 1.1 slice_bitcast_fusion
  151.2 1.3 slice.17
  152.5 4.8 %all-to-all-done.4 = f32[32,1,128]{2,1,0:T(1,128)S(1)} async-done(((f32[32,1,128]{2,1,0:T(1,128)}), f32[32,1,128]{2,1,0:T(1,128)S(1)}, u32[]{:S(2)}, u32[]{:S(2)}) %all-to-all-start.4) | async-done | bytes 16416 | tf_op jit(solution)/shard_map/all_to_all | solution.py:568
  157.2 0.6 slice_reduce_fusion
  158.5 1.3 pad_maximum_fusion.2
  (2 shorter events, 0.0 us)
Async XLA Ops:
  0.6 19.5 %copy-start = (f32[3,8,8,256]{3,2,1,0:T(8,128)S(1)}, f32[3,8,8,256]{3,2,1,0:T(8,128)}, u32[]{:S(2)}) copy-start(f32[3,8,8,256]{3,2,1,0:T(8,128)} %lanczos.3) | copy-start | bytes 589828
  2.4 18.6 %copy-start.5 = (f32[13,3,3]{0,2,1:T(4,128)S(1)}, f32[13,3,3]{0,2,1:T(4,128)}, u32[]{:S(2)}) copy-start(f32[13,3,3]{0,2,1:T(4,128)} %param.14) | copy-start | bytes 1408
  3.5 6.4 %collective-permute-start = (f32[4,7,8,256]{3,2,1,0:T(8,128)S(1)}, f32[4,7,8,256]{3,2,1,0:T(8,128)S(1)}, u32[]{:S(2)}, u32[]{:S(2)}) collective-permute-start(f32[4,7,8,256]{3,2,1,0:T(8,128)S(1)} %get-tuple-element.55), channel_id=1, source_target_pairs={{8,16},{16,8},{9,17},{17,9},{10,18},{18,10},{11,19},{19,11},{12,20... | collective-permute-start | bytes 688136 | tf_op jit(solution)/shard_map/ppermute | solution.py:594
  4.2 15.9 %collective-permute-start.1 = (f32[4,7,8,256]{3,2,1,0:T(8,128)S(1)}, f32[4,7,8,256]{3,2,1,0:T(8,128)S(1)}, u32[]{:S(2)}, u32[]{:S(2)}) collective-permute-start(f32[4,7,8,256]{3,2,1,0:T(8,128)S(1)} %get-tuple-element.56), channel_id=1, source_target_pairs={{0,8},{8,0},{16,24},{24,16},{1,9},{9,1},{17,25},{25,17},{2,10},{10... | collective-permute-start | bytes 688136 | tf_op jit(solution)/shard_map/ppermute | solution.py:593
  20.2 2.3 %copy-start.1 = (f32[4,22,8,256]{3,2,1,0:T(8,128)}, f32[4,22,8,256]{3,2,1,0:T(8,128)S(1)}, u32[]{:S(2)}) copy-start(f32[4,22,8,256]{3,2,1,0:T(8,128)S(1)} %pad_maximum_fusion.mid) | copy-start | bytes 2162692
  20.2 2.3 %collective-permute-start.2 = (f32[4,22,8,256]{3,2,1,0:T(8,128)S(1)}, f32[4,22,8,256]{3,2,1,0:T(8,128)S(1)}, u32[]{:S(2)}, u32[]{:S(2)}) collective-permute-start(f32[4,22,8,256]{3,2,1,0:T(8,128)S(1)} %pad_maximum_fusion.mid), channel_id=1, source_target_pairs={{0,1},{1,0},{2,3},{3,2},{4,5},{5,4},{6,7},{7,6},{8,9},{9,8},{10,11... | collective-permute-start | bytes 2162696 | tf_op jit(solution)/shard_map/ppermute | solution.py:599
  20.3 2.2 %collective-permute-start.3 = (f32[4,22,8,256]{3,2,1,0:T(8,128)S(1)}, f32[4,22,8,256]{3,2,1,0:T(8,128)S(1)}, u32[]{:S(2)}, u32[]{:S(2)}) collective-permute-start(f32[4,22,8,256]{3,2,1,0:T(8,128)S(1)} %pad_maximum_fusion.mid), channel_id=1, source_target_pairs={{1,2},{2,1},{3,4},{4,3},{5,6},{6,5},{9,10},{10,9},{11,12},{12,11},... | collective-permute-start | bytes 2162696 | tf_op jit(solution)/shard_map/ppermute | solution.py:600
  22.5 0.9 copy-start.2
  23.4 0.9 copy-start.3
  109.5 9.7 %all-to-all-start.2 = ((f32[32,1,128]{2,1,0:T(1,128)}), f32[32,1,128]{2,1,0:T(1,128)S(1)}, u32[]{:S(2)}, u32[]{:S(2)}) async-start(f32[32,1,128]{2,1,0:T(1,128)} %bitcast.43), calls=%async_computation.2 | async-start | bytes 32768 | tf_op jit(solution)/shard_map/all_to_all | solution.py:568
  119.2 0.6 copy-start.4
  147.6 9.7 %all-to-all-start.4 = ((f32[32,1,128]{2,1,0:T(1,128)}), f32[32,1,128]{2,1,0:T(1,128)S(1)}, u32[]{:S(2)}, u32[]{:S(2)}) async-start(f32[32,1,128]{2,1,0:T(1,128)} %bitcast.42), calls=%async_computation.4 | async-start | bytes 32768 | tf_op jit(solution)/shard_map/all_to_all | solution.py:568

commit v2 on v1

v2 whole, which is shorter than its diff:
```python
import functools

import jax
import jax.numpy as jnp
from jax import lax
from jax.experimental import pallas as pl
from jax.experimental.pallas import tpu as pltpu
from jax.sharding import PartitionSpec as P

BRICK = 8
ITERS = 3
SHIFT_MASS = 0.02
SMOOTH_WEIGHT = 0.5
VOID_DENSITY = 0.1

AXES = ("slab", "block")
LANES = 128
WIDE = (8, 24)
MID = (4, 16)
OWN = (0, 8)
REACH = 2 * ITERS
PAIRS = [(n // 9 - 1, n // 3 % 3 - 1, n % 3 - 1) for n in range(13)]
f32 = jnp.float32


def along_z(field, dz):
    rows, depth = field.shape
    lane = lax.broadcasted_iota(jnp.int32, (rows, LANES), 1)
    chunks = [field[:, low : low + LANES] for low in range(0, depth, LANES)]
    turned = [pltpu.roll(chunk, (-dz) % LANES, 1) for chunk in chunks]
    edge = 0 if dz < 0 else LANES - 1
    out = []
    for number, chunk in enumerate(turned):
        other = number + dz
        filler = turned[other] if 0 <= other < len(turned) else 0.0
        out.append(jnp.where(lane == edge, filler, chunk))
    return jnp.concatenate(out, axis=1)


def shift_store(dest, at, fields, source, target):
    src_off, src_rows = source
    dst_off, dst_rows = target
    for comp, field in enumerate(fields):
        for dy in (-1, 0, 1):
            shift = src_off - dst_off + dy
            moved = field if shift == 0 else pltpu.roll(field, (-shift) % src_rows, 0)
            if dst_rows != src_rows:
                moved = moved[:dst_rows]
            for dz in (-1, 0, 1):
                out = moved if dz == 0 else along_z(moved, dz)
                dest[((dy + 1) * 3 + dz + 1) * len(fields) + comp, at] = out


def pair_slots(pair):
    dx, dy, dz = pair
    return dx, (dy + 1) * 3 + dz + 1, (1 - dy) * 3 + 1 - dz


def stencil(moved, at, coup, center):
    near = [moved[4 * 3 + c, at] for c in range(3)]
    total = [center(i) * value for i, value in enumerate(six_of(near))]
    for number, pair in enumerate(PAIRS):
        dx, plus, minus = pair_slots(pair)
        sums = [moved[plus * 3 + c, at + dx] + moved[minus * 3 + c, at - dx] for c in range(3)]
        for i, value in enumerate(six_of(sums)):
            total[i] = total[i] + coup[number * 6 + i] * value
    out = [
        total[0] + (total[3] + total[4]),
        total[1] + (total[3] + total[5]),
        total[2] + (total[4] + total[5]),
    ]
    return out, near


def six_of(three):
    return [*three, three[0] + three[1], three[0] + three[2], three[1] + three[2]]


def loop(low, high, body):
    def step(i, carry):
        body(i)
        return carry

    lax.fori_loop(low, high, step, 0)


def row_sum(x):
    return jnp.sum(x, axis=0, keepdims=True)


def to_lanes(rows):
    column = jnp.sum(rows, axis=1, keepdims=True)
    count = rows.shape[0]
    here = lax.broadcasted_iota(jnp.int32, (count, LANES), 0)
    lane = lax.broadcasted_iota(jnp.int32, (count, LANES), 1)
    return row_sum(jnp.where(here == lane, column, 0.0))


def pick(row, index):
    lane = lax.broadcasted_iota(jnp.int32, row.shape, 1)
    return jnp.sum(jnp.where(lane == index, row, 0.0), axis=1, keepdims=True)


def scalar(one):
    return one[0, 0]


def coarse_values(means, rows_of, where, counts, store):
    total = None
    for k in range(3):
        part = row_sum(rows_of(k) * means[:, k : k + 1])
        total = part if total is None else total + part
    for bx in range(3):
        for by in range(3):
            spot = (where[0] + bx - 1) * counts[1] + where[1] + by - 1
            for k in range(3):
                store[(bx * 3 + by) * 3 + k] = scalar(pick(total, spot * 3 + k))


def correction(store, x, k, layout, span, depth):
    off, rows = layout
    base = lax.div(x + span, span) * 9 + k
    row = lax.broadcasted_iota(jnp.int32, (rows, depth), 0)
    high = jnp.where(row < off + 8, store[base + 3], store[base + 6])
    return jnp.where(row < off, store[base], high)


def send(msg, low, row, count):
    width = row.shape[1]
    msg[:, :, low : low + width] = jnp.broadcast_to(row.reshape(1, 1, width), (count, 1, width))


def side_rows(where, even, odd, mid):
    flip = where[1] % 2 == 1

    def wide(comp, x):
        first, second = even[comp, x], odd[comp, x]
        low = jnp.where(flip, first, second)
        high = jnp.where(flip, second, first)
        return jnp.concatenate([low, mid[comp, x], high], axis=0)

    return wide


def repack(field):
    return pltpu.roll(field, WIDE[1] - (WIDE[0] - MID[0]), 0)[: MID[1]]


def own_of(field):
    return pltpu.roll(field, MID[1] - MID[0], 0)[:8]


def center_row(moved_root, at, root, coup):
    total = [None] * 6
    for number, pair in enumerate(PAIRS):
        dx, plus, minus = pair_slots(pair)
        both = moved_root[plus, at + dx] + moved_root[minus, at - dx]
        for i in range(6):
            term = coup[number * 6 + i] * both
            total[i] = term if total[i] is None else total[i] + term
    inside = root > 0.0
    inverse = jnp.where(inside, 1.0 / jnp.where(inside, root, 1.0), 0.0)
    center = [-total[i] * inverse for i in range(6)]
    center[:3] = [one + SHIFT_MASS for one in center[:3]]
    whole = [
        center[0] + (center[3] + center[4]),
        center[1] + (center[3] + center[5]),
        center[2] + (center[4] + center[5]),
    ]
    half = [jnp.where(inside, SMOOTH_WEIGHT / one, 0.0) for one in whole]
    return center, half, inverse


def setup_kernel(
    dims, where, coup, even, odd, mid, cinv,
    kh_w, h_w, v_w, root_w, kh_m, h_m, v_m, root_m, kh_o, v_o, root_o, msg,
    moved_root, root_all, moved_own, sums,
):
    span, depth, devices = dims
    halo = REACH + 1
    wide = side_rows(where, even, odd, mid)

    def roots(x):
        root = jnp.sqrt(wide(3, x))
        root_all[x] = root
        shift_store(moved_root, x, [root], WIDE, WIDE)

    def diagonals(x, also_mid, also_own):
        at = x + 1
        root = root_all[at]
        center, half, inverse = center_row(moved_root, at, root, coup)
        m, o = x - (REACH - 4), x - REACH
        vectors = [wide(k, at) * inverse for k in range(3)]
        root_w[x] = root
        for k in range(3):
            h_w[k, x] = half[k]
            v_w[k, x] = vectors[k]
        for i in range(6):
            kh_w[i, x] = center[i]
        if also_mid:
            root_m[m] = repack(root)
            for k in range(3):
                h_m[k, m] = repack(half[k])
                v_m[k, m] = repack(vectors[k])
            for i in range(6):
                kh_m[i, m] = repack(center[i])
        if also_own:
            own = slice(WIDE[0], WIDE[0] + 8)
            root_o[o] = root[own]
            for k in range(3):
                v_o[k, o] = vectors[k][own]
            for i in range(6):
                kh_o[i, o] = center[i][own]

    loop(0, span + 2 * halo, roots)

    def both(also_mid, also_own):
        def body(x):
            diagonals(x, also_mid, also_own)

        return body

    edge = REACH - 4
    loop(0, edge, both(False, False))
    loop(edge, REACH, both(True, False))
    loop(REACH, REACH + span, both(True, True))
    loop(REACH + span, edge + span + 8, both(True, False))
    loop(edge + span + 8, span + 2 * REACH, both(False, False))

    def smooth(x):
        at = x + REACH - 1
        shift_store(moved_own, x, [h_w[k, at] * v_w[k, at] for k in range(3)], WIDE, OWN)

    loop(0, span + 2, smooth)

    def remain(x, carry):
        for i in (2 * x, 2 * x + 1):
            image, _ = stencil(moved_own, i + 1, coup, lambda slot: kh_o[slot, i])
            carry = tuple(carry[k] + root_o[i] * (v_o[k, i] - image[k]) for k in range(3))
        return carry

    zero = jnp.zeros((8, depth), f32)
    parts = lax.fori_loop(0, span // 2, remain, (zero, zero, zero))
    sums[...] = jnp.zeros_like(sums)
    for k in range(3):
        sums[k : k + 1] = row_sum(parts[k])
    send(msg, 0, to_lanes(sums[...]) * (1.0 / (span * 8 * depth)), devices)
    width = cinv.shape[1]
    padded = (msg.shape[2] - LANES) // 3
    for k in range(3):
        row = cinv[k : k + 1]
        if padded != width:
            row = jnp.concatenate([row, jnp.zeros((1, padded - width), f32)], axis=1)
        send(msg, LANES + k * padded, row, devices)


def iterate(dims, level, layouts, coup, store, residual, half, root, center, moved, moved_next, z_all, image):
    span, depth = dims
    source, first, second = layouts

    def begin(x):
        fields = []
        for k in range(3):
            fix = correction(store, x - level, k, source, span, depth)
            fields.append(half(k, x) * residual(k, x) + root(x) * fix)
        shift_store(moved, x, fields, source, first)

    def middle(x):
        at = x + 1
        out, near = stencil(moved, at, coup, center(at))
        fields = [near[k] + half(k, at) * (residual(k, at) - out[k]) for k in range(3)]
        for k in range(3):
            z_all[k, x] = fields[k]
        shift_store(moved_next, x, fields, first, second)

    def both(x):
        begin(x + 2)
        middle(x)

    loop(0, span + 2 * level, begin)
    loop(0, span + 2 * level - 2, middle)
    if image is not None:
        loop(0, span + 2 * level - 4, image)


def own_rows(layout):
    return slice(layout[0], layout[0] + 8)


def means_of(dims, coup, root, half, mapped, center, moved_own):
    span, depth = dims

    def begin(x):
        shift_store(moved_own, x, [half(k, x) * mapped(k, x) for k in range(3)], MID, OWN)

    def body(x, carry):
        for i in (2 * x, 2 * x + 1):
            image, _ = stencil(moved_own, i + 1, coup, lambda slot: center(slot, i))
            carry = tuple(carry[k] + root(i) * (own_of(mapped(k, i + 1)) - image[k]) for k in range(3))
        return carry

    loop(0, span + 2, begin)
    zero = jnp.zeros((8, depth), f32)
    return lax.fori_loop(0, span // 2, body, (zero, zero, zero))


def first_kernel(
    dims, counts, where, coup, got, kh_w, h_w, v_w, root_w, kh_m, h_m, kh_o, v_o, root_o,
    z_own, mapped, msg,
    moved, moved_next, moved_own, z_all, store, sums,
):
    span, depth, devices = dims
    level = REACH
    padded = (got.shape[2] - LANES) // 3
    coarse_values(
        got[:, 0, :LANES],
        lambda k: got[:, 0, LANES + k * padded : LANES + (k + 1) * padded],
        where, counts, store,
    )

    def image(x):
        out, _ = stencil(moved_next, x + 1, coup, lambda i: kh_m[i, x])
        for k in range(3):
            mapped[k, x] = out[k]

    iterate(
        (span, depth), level, (WIDE, WIDE, MID), coup, store,
        lambda k, x: v_w[k, x], lambda k, x: h_w[k, x], lambda x: root_w[x],
        (lambda at: lambda i: kh_w[i, at]), moved, moved_next, z_all, image,
    )
    inner = level - 2
    parts = means_of(
        (span, depth), coup, lambda x: root_o[x],
        lambda k, x: h_m[k, x + 3], lambda k, x: mapped[k, x + inner - 1],
        lambda i, x: kh_o[i, x], moved_own,
    )

    def dots(x, carry):
        gamma, delta = carry
        for k in range(3):
            z = z_all[k, x + level - 1, own_rows(WIDE)]
            z_own[k, x] = z
            gamma = gamma + v_o[k, x] * z
            delta = delta + own_of(mapped[k, x + inner]) * z
        return gamma, delta

    zero = jnp.zeros((8, depth), f32)
    gamma, delta = lax.fori_loop(0, span, dots, (zero, zero))
    scale = 1.0 / (span * 8 * depth)
    sums[...] = jnp.zeros_like(sums)
    for k in range(3):
        sums[k : k + 1] = row_sum(parts[k]) * scale
    sums[3:4] = row_sum(gamma)
    sums[4:5] = row_sum(delta)
    send(msg, 0, to_lanes(sums[...]), devices)


def second_kernel(
    dims, counts, where, coup, got, first, kh_m, h_m, v_m, root_m, kh_o, root_o, mapped_old,
    z_own, mapped, residual, means, msg,
    moved, moved_next, moved_own, z_all, store, sums,
):
    span, depth, devices = dims
    level = REACH - 2
    total = row_sum(got[:, 0])
    gamma = pick(total, 3)
    step = gamma / pick(total, 4)
    padded = (first.shape[2] - LANES) // 3
    fresh = first[:, 0, :LANES] - step * got[:, 0]
    means[...] = fresh
    coarse_values(
        fresh,
        lambda k: first[:, 0, LANES + k * padded : LANES + (k + 1) * padded],
        where, counts, store,
    )
    size = scalar(step)

    def rest(k, x):
        return v_m[k, x] - size * mapped_old[k, x]

    def image(x):
        out, _ = stencil(moved_next, x + 1, coup, lambda i: kh_m[i, x + 2])
        for k in range(3):
            mapped[k, x] = out[k]

    iterate(
        (span, depth), level, (MID, MID, MID), coup, store,
        rest, lambda k, x: h_m[k, x], lambda x: root_m[x],
        (lambda at: lambda i: kh_m[i, at]), moved, moved_next, z_all, image,
    )
    inner = level - 2
    parts = means_of(
        (span, depth), coup, lambda x: root_o[x],
        lambda k, x: h_m[k, x + 3], lambda k, x: mapped[k, x + inner - 1],
        lambda i, x: kh_o[i, x], moved_own,
    )

    def dots(x, carry):
        gamma, delta, cross = carry
        for k in range(3):
            z = own_of(z_all[k, x + level - 1])
            z_own[k, x] = z
            gamma = gamma + own_of(rest(k, x + level)) * z
            delta = delta + own_of(mapped[k, x + inner]) * z
            cross = cross + own_of(mapped_old[k, x + 4]) * z
        return gamma, delta, cross

    zero = jnp.zeros((8, depth), f32)
    dotted = lax.fori_loop(0, span, dots, (zero, zero, zero))

    def keep(x):
        for k in range(3):
            residual[k, x] = rest(k, x + inner)

    loop(0, span + 2 * inner, keep)
    scale = 1.0 / (span * 8 * depth)
    sums[...] = jnp.zeros_like(sums)
    for k in range(3):
        sums[k : k + 1] = row_sum(parts[k]) * scale
        sums[k + 3 : k + 4] = row_sum(dotted[k])
    send(msg, 0, to_lanes(sums[...]), devices)


def third_kernel(
    dims, counts, where, coup, got, got_old, first, means, kh_m, h_m, root_m, kh_o, v_o, root_o,
    z_old, mapped_old, z_new, mapped_new, residual_old, lanczos, previous, locked,
    base, z_out, dir_out, scal, msg,
    moved, moved_next, residual, mapped, z_all, store, sums, locked_sums,
):
    span, depth, devices = dims
    level = REACH - 4
    total_old = row_sum(got_old[:, 0])
    total = row_sum(got[:, 0])
    gamma_old = pick(total_old, 3)
    delta_old = pick(total_old, 4)
    step_old = gamma_old / delta_old
    gamma = pick(total, 3)
    ratio = gamma / gamma_old
    delta = pick(total, 4) + 2.0 * ratio * pick(total, 5) + ratio * ratio * delta_old
    step = gamma / delta
    fresh = means[...] - step * (got[:, 0] + ratio * got_old[:, 0])
    padded = (first.shape[2] - LANES) // 3
    coarse_values(
        fresh,
        lambda k: first[:, 0, LANES + k * padded : LANES + (k + 1) * padded],
        where, counts, store,
    )
    lane = lax.broadcasted_iota(jnp.int32, (1, LANES), 1)
    scal[...] = jnp.where(lane == 0, gamma, jnp.where(lane == 1, delta, 0.0))
    size, size_old, blend = scalar(step), scalar(step_old), scalar(ratio)

    def update(x):
        for k in range(3):
            mapped[k, x] = mapped_new[k, x] + blend * mapped_old[k, x + 2]
            residual[k, x] = residual_old[k, x] - size * mapped[k, x]

    loop(0, span + 2 * level, update)
    iterate(
        (span, depth), level, (MID, MID, OWN), coup, store,
        lambda k, x: residual[k, x], lambda k, x: h_m[k, x + 2], lambda x: root_m[x + 2],
        (lambda at: lambda i: kh_m[i, at + 2]), moved, moved_next, z_all, None,
    )

    def finish(x, carry):
        gamma, delta, cross, with_base, with_z, with_dir, weight = carry
        image, near = stencil(moved_next, x + 1, coup, lambda i: kh_o[i, x])
        inverse = 1.0 / root_o[x]
        for k in range(3):
            z = near[k]
            direction = z_new[k, x] + blend * z_old[k, x]
            partial = size_old * z_old[k, x] + size * direction
            vector = v_o[k, x]
            gamma = gamma + own_of(residual[k, x + level]) * z
            delta = delta + image[k] * z
            cross = cross + own_of(mapped[k, x + level]) * z
            with_base = with_base + vector * partial
            with_z = with_z + vector * z
            with_dir = with_dir + vector * direction
            weight = weight + lanczos[k, x] * lanczos[k, x]
            z_out[k, x] = z * inverse
            dir_out[k, x] = direction * inverse
            base[k, x] = partial * inverse - coup[6 * len(PAIRS)] * previous[k, x]
        return gamma, delta, cross, with_base, with_z, with_dir, weight

    zero = jnp.zeros((8, depth), f32)
    dotted = lax.fori_loop(0, span, finish, (zero,) * 7)
    sums[...] = jnp.zeros_like(sums)
    for k in range(7):
        sums[k : k + 1] = row_sum(dotted[k])

    def project(n):
        def body(x, carry):
            out = list(carry)
            for k in range(3):
                vector = locked[n, k, x]
                out[0] = out[0] + vector * base[k, x]
                out[1] = out[1] + vector * z_out[k, x]
                out[2] = out[2] + vector * dir_out[k, x]
                out[3] = out[3] + vector * lanczos[k, x]
            return tuple(out)

        four = lax.fori_loop(0, span, body, (zero,) * 4, unroll=True)
        rows = [row_sum(one) for one in four]
        locked_sums[n] = jnp.concatenate(rows, axis=0)

    count = locked.shape[0]
    loop(0, count, project)
    send(msg, 0, to_lanes(sums[...]), devices)
    flat = locked_sums[...].reshape(count * 4, depth)
    send(msg, LANES, to_lanes(flat), devices)


def last_kernel(
    dims, got, scal, base, z, direction, lanczos, locked,
    remainder, weights, found, msg,
    sums,
):
    span, depth, devices = dims
    count = locked.shape[0]
    total = row_sum(got[:, 0])
    head, tail = total[:, :LANES], total[:, LANES:]
    gamma_old, delta_old = pick(scal[...], 0), pick(scal[...], 1)
    gamma = pick(head, 0)
    ratio = gamma / gamma_old
    delta = pick(head, 1) + 2.0 * ratio * pick(head, 2) + ratio * ratio * delta_old
    step = gamma / delta
    inner = pick(head, 3) + step * (pick(head, 4) + ratio * pick(head, 5))
    alpha = inner / pick(head, 6)
    lane = lax.broadcasted_iota(jnp.int32, (1, LANES), 1)
    kind = lane % 4
    factor = jnp.where(kind == 0, 1.0, jnp.where(kind == 1, step, jnp.where(kind == 2, step * ratio, -alpha)))
    terms = jnp.where(lane < 4 * count, tail * factor, 0.0)
    for n in range(count):
        value = jnp.sum(jnp.where(lane // 4 == n, terms, 0.0), axis=1, keepdims=True)
        weights[n] = scalar(value)
    found[0] = scalar(alpha)
    size, both, shrink = scalar(step), scalar(step * ratio), scalar(alpha)

    def body(x, square):
        for k in range(3):
            rest = base[k, x] + size * z[k, x] + both * direction[k, x] - shrink * lanczos[k, x]
            taken = weights[0] * locked[0, k, x]
            for n in range(1, count):
                taken = taken + weights[n] * locked[n, k, x]
            rest = rest - taken
            remainder[k, x] = rest
            square = square + rest * rest
        return square

    square = lax.fori_loop(0, span, body, jnp.zeros((8, depth), f32))
    sums[...] = jnp.zeros_like(sums)
    sums[0:1] = row_sum(square)
    send(msg, 0, to_lanes(sums[...]), devices)


def closing_kernel(cells, got, found, out):
    total = jnp.sum(row_sum(got[:, 0])[:, :8], axis=1, keepdims=True)
    out[0] = found[0]
    out[1] = scalar(jnp.sqrt(total / cells))


VMEM = pl.BlockSpec(memory_space=pltpu.VMEM)
SMEM = pl.BlockSpec(memory_space=pltpu.SMEM)


def call(kernel, name, outs, scratch, *operands, limit=60 << 20):
    return pl.pallas_call(
        kernel,
        name=name,
        out_shape=[jax.ShapeDtypeStruct(shape, f32) for shape in outs],
        in_specs=[SMEM if len(operand.shape) == 1 else VMEM for operand in operands],
        out_specs=[SMEM if len(shape) == 1 else VMEM for shape in outs],
        scratch_shapes=scratch,
        compiler_params=pltpu.CompilerParams(vmem_limit_bytes=limit),
    )(*operands)


def swap_permutes(axis):
    count = lax.axis_size(axis)
    near = [(i, i ^ 1) for i in range(count) if i ^ 1 < count]
    far = [(i, ((i + 1) ^ 1) - 1) for i in range(count)]
    return near, [(i, j) for i, j in far if 0 <= j < count]


def exchange_rows(rows):
    return lax.all_to_all(rows, AXES, 0, 0, tiled=True)


def shards(
    lanczos_vector, previous_vector, previous_beta, locked_vectors, occupancy, young, couplings, coarse_inverse
):
    _, span, span_y, depth = lanczos_vector.shape
    counts = (lax.axis_size("slab"), lax.axis_size("block"))
    devices = counts[0] * counts[1]
    locked = locked_vectors.shape[0]
    halo = REACH + 1
    assert span_y == 8 and span >= halo and locked * 4 <= LANES
    slab, block = lax.axis_index("slab"), lax.axis_index("block")
    where = jnp.stack([slab, block]).astype(jnp.int32)
    flat = -couplings.reshape(-1, 9)
    a, b, c = flat[:, 1], flat[:, 2], flat[:, 5]
    six = jnp.stack([flat[:, 0] - a - b, flat[:, 4] - a - c, flat[:, 8] - b - c, a, b, c], axis=1)
    coup = jnp.concatenate([six.reshape(-1), previous_beta.reshape(1)])

    density = jnp.where(occupancy == 1, 1.0, VOID_DENSITY).astype(f32)
    density = jnp.repeat(jnp.repeat(jnp.repeat(density, BRICK, 0), BRICK, 1), BRICK, 2)
    stiffness = density * young
    fields = jnp.concatenate([lanczos_vector, stiffness[None]], axis=0)

    odd = slab % 2
    near, far = swap_permutes("slab")
    upper = lax.slice_in_dim(fields, span - halo, span, axis=1)
    lower = lax.slice_in_dim(fields, 0, halo, axis=1)
    from_near = lax.ppermute(jnp.where(odd == 0, upper, lower), "slab", near)
    from_far = lax.ppermute(jnp.where(odd == 0, lower, upper), "slab", far)
    below = jnp.where(odd == 0, from_far, from_near)
    above = jnp.where(odd == 0, from_near, from_far)
    tall = jnp.concatenate([below, fields, above], axis=1)
    near, far = swap_permutes("block")
    tall, where, coup, coarse_inverse = lax.optimization_barrier((tall, where, coup, coarse_inverse))
    side_near = lax.ppermute(tall, "block", near)
    side_far = lax.ppermute(tall, "block", far)

    dims = (span, depth, devices)
    wide = (span + 2 * REACH, WIDE[1], depth)
    mid = (span + 8, MID[1], depth)
    own = (3, span, 8, depth)
    padded = -(-coarse_inverse.shape[1] // LANES) * LANES
    row = (devices, 1, LANES)

    def scratch(*shape):
        return pltpu.VMEM(shape, f32)

    kh_w, h_w, v_w, root_w, kh_m, h_m, v_m, root_m, kh_o, v_o, root_o, msg = call(
        functools.partial(setup_kernel, dims),
        "setup",
        [
            (6, *wide), (3, *wide), (3, *wide), wide, (6, *mid), (3, *mid), (3, *mid), mid,
            (6, *own[1:]), own, own[1:], (devices, 1, LANES + 3 * padded),
        ],
        [
            scratch(9, span + 2 * halo + 1, WIDE[1], depth),
            scratch(span + 2 * halo + 1, WIDE[1], depth),
            scratch(27, span + 2, 8, depth),
            scratch(8, depth),
        ],
        where, coup, side_near, side_far, tall, coarse_inverse, limit=9 << 20,
    )
    first = exchange_rows(msg)

    store = pltpu.SMEM((27,), f32)
    z_0, mapped_0, msg = call(
        functools.partial(first_kernel, dims, counts),
        "first",
        [own, (3, *mid), row],
        [
            scratch(27, *wide),
            scratch(27, span + 2 * REACH - 2, MID[1], depth),
            scratch(27, span + 2, 8, depth),
            scratch(3, span + 2 * REACH - 2, WIDE[1], depth),
            store,
            scratch(8, depth),
        ],
        where, coup, first, kh_w, h_w, v_w, root_w, kh_m, h_m, kh_o, v_o, root_o, limit=28 << 20,
    )
    got_0 = exchange_rows(msg)

    level = REACH - 2
    inner = (3, span + 2 * level - 4, MID[1], depth)
    z_1, mapped_1, residual, means, msg = call(
        functools.partial(second_kernel, dims, counts),
        "second",
        [own, inner, inner, (devices, LANES), row],
        [
            scratch(27, *mid),
            scratch(27, span + 2 * level - 2, MID[1], depth),
            scratch(27, span + 2, 8, depth),
            scratch(3, span + 2 * level - 2, MID[1], depth),
            store,
            scratch(8, depth),
        ],
        where, coup, got_0, first, kh_m, h_m, v_m, root_m, kh_o, root_o, mapped_0, limit=18 << 20,
    )
    got_1 = exchange_rows(msg)

    level = REACH - 4
    base, z_2, direction, scal, msg = call(
        functools.partial(third_kernel, dims, counts),
        "third",
        [own, own, own, (1, LANES), (devices, 1, 2 * LANES)],
        [
            scratch(27, span + 2 * level, MID[1], depth),
            scratch(27, span + 2 * level - 2, 8, depth),
            scratch(3, span + 2 * level, MID[1], depth),
            scratch(3, span + 2 * level, MID[1], depth),
            scratch(3, span + 2 * level - 2, MID[1], depth),
            store,
            scratch(8, depth),
            scratch(locked, 4, depth),
        ],
        where, coup, got_1, got_0, first, means, kh_m, h_m, root_m, kh_o, v_o, root_o,
        z_0, mapped_0, z_1, mapped_1, residual, lanczos_vector, previous_vector, locked_vectors, limit=16 << 20,
    )
    got_2 = exchange_rows(msg)

    remainder, projections, found, msg = call(
        functools.partial(last_kernel, dims),
        "last",
        [own, (locked,), (1,), row],
        [scratch(8, depth)],
        got_2, scal, base, z_2, direction, lanczos_vector, locked_vectors, limit=6 << 20,
    )
    (coefficients,) = call(
        functools.partial(closing_kernel, 3.0 * span * span_y * depth * devices),
        "closing",
        [(2,)],
        [],
        exchange_rows(msg), found, limit=4 << 20,
    )
    return remainder, coefficients, projections


def solution(mesh):
    in_specs = (
        P(None, "slab", "block", None),
        P(None, "slab", "block", None),
        P(),
        P(None, None, "slab", "block", None),
        P("slab", "block", None),
        P("slab", "block", None),
        P(),
        P(("slab", "block"), None),
    )
    out_specs = (P(None, "slab", "block", None), P(), P())
    return jax.shard_map(shards, mesh=mesh, in_specs=in_specs, out_specs=out_specs, check_vma=False)
```

time: 160 us -> 130 us (0.81)
  Pallas kernels: 69.4 us -> 49.6 us
  blocking collectives: 40.7 us -> 54.7 us
  waiting for transfers between devices: 21.5 us -> 10.2 us
  local copies, waits for them, and re-layouts: 8.6 us -> 0.4 us
  starting transfers between devices: 12.2 us -> 10.1 us
  other arithmetic: 5.29 us -> 3.66 us
    pallas_call x5 -> x6, Pallas kernels: 69.4 us -> 49.6 us  [call(): pl.pallas_call(kernel, name=name, out_shape=[jax.ShapeDtypeStruct(shape,...]
    all_to_all x3 -> x5, blocking collectives: 40.7 us -> 54.7 us  [exchange_rows(): return lax.all_to_all(rows, AXES, 0, 0, tiled=True)]
    all_to_all x2 -> x0, waiting for transfers between devices: 11.3 us -> none  [exchange_rows(): return lax.all_to_all(rows, AXES, 0, 0, tiled=True)]
    all_to_all x2 -> x0, starting transfers between devices: 5 us -> none  [exchange_rows(): return lax.all_to_all(rows, AXES, 0, 0, tiled=True)]
    unnamed x15 -> x8, local copies, waits for them, and re-layouts: 3.72 us -> 0.02 us
    ppermute x1, starting transfers between devices: 0.07 us -> 2.96 us  [shards(): side_near = lax.ppermute(tall, 'block', near)]
    ppermute x1, waiting for transfers between devices: 0.06 us -> 1.81 us  [shards(): side_near = lax.ppermute(tall, 'block', near)]
    ppermute x1, waiting for transfers between devices: 10.1 us -> 8.41 us  [shards(): from_near = lax.ppermute(jnp.where(odd == 0, upper, lower), 'slab', near)]
  transfers between devices with their start and end apart: 6 -> 4, of which waited for: 4 -> 2; matrix products, arithmetic and copies ran while one was open for 2% -> 1% of each run, Pallas kernels for 0% -> 0%
where the time goes in v2:
time: 130 us
  blocking collectives  54.7 us (42%)
  Pallas kernels  49.6 us (38%)
  waiting for transfers between devices  10.2 us (8%)
  starting transfers between devices  10.1 us (8%)
  other arithmetic  3.66 us (3%)
  between operations  1.39 us (1%)
    all_to_all x5, blocking collectives, exchange_rows(): return lax.all_to_all(rows, AXES, 0, 0, tiled=True)  54.7 us
    pallas_call x6, Pallas kernels, call(): pl.pallas_call(kernel, name=name, out_shape=[jax.ShapeDtypeStruct(shape,...  49.6 us
    ppermute x1, waiting for transfers between devices, shards(): from_near = lax.ppermute(jnp.where(odd == 0, upper, lower), 'slab', near)  8.41 us
    ppermute x1, starting transfers between devices, shards(): from_near = lax.ppermute(jnp.where(odd == 0, upper, lower), 'slab', near)  5.76 us
    ppermute x1, starting transfers between devices, shards(): side_near = lax.ppermute(tall, 'block', near)  2.96 us
  transfers between devices with their start and end apart: 4, of which 2 were waited for; matrix products, arithmetic and copies ran while one was open for 1% of the time, Pallas kernels for 0%

profile of v2, /device:TPU:0, one launch (start us, length us, event | category | flops | bytes accessed | tf_op | source)
XLA Modules:
  0.0 130.1 jit_solution(11081261534337735673)
XLA Ops:
  0.6 0.0 copy-start.1
  0.7 0.7 fusion.3
  1.4 0.1 broadcast_in_dim.22
  1.4 0.1 broadcast_in_dim.23
  1.5 0.9 multiply_bitcast_fusion
  2.4 0.0 copy-start.3
  2.4 1.2 fusion.1
  3.5 0.7 collective-permute-start
  4.2 5.8 %collective-permute-start.1 = (f32[4,7,8,256]{3,2,1,0:T(8,128)S(1)}, f32[4,7,8,256]{3,2,1,0:T(8,128)S(1)}, u32[]{:S(2)}, u32[]{:S(2)}) collective-permute-start(f32[4,7,8,256]{3,2,1,0:T(8,128)S(1)} %get-tuple-element.72), channel_id=1, source_target_pairs={{0,8},{8,0},{16,24},{24,16},{1,9},{9,1},{17,25},{25,17},{2,10},{10... | collective-permute-start | bytes 688136 | tf_op jit(solution)/shard_map/ppermute | solution.py:614
  10.0 0.7 neg.6
  11.4 0.1 copy.12
  11.5 0.1 reshape.19
  11.6 0.1 pad_add_fusion.where
  11.6 0.1 pad_maximum_fusion.2.coup
  11.7 0.0 collective-permute-done
  11.7 8.4 %collective-permute-done.1 = f32[4,7,8,256]{3,2,1,0:T(8,128)S(1)} collective-permute-done((f32[4,7,8,256]{3,2,1,0:T(8,128)S(1)}, f32[4,7,8,256]{3,2,1,0:T(8,128)S(1)}, u32[]{:S(2)}, u32[]{:S(2)}) %collective-permute-start.1) | collective-permute-done | bytes 229408 | tf_op jit(solution)/shard_map/ppermute | solution.py:614
  20.2 0.0 copy-done.1
  20.2 0.1 pad_maximum_fusion.mid
  20.2 0.7 collective-permute-start.3
  20.9 3.0 %collective-permute-start.2 = (f32[4,22,8,256]{3,2,1,0:T(8,128)S(1)}, f32[4,22,8,256]{3,2,1,0:T(8,128)S(1)}, u32[]{:S(2)}, u32[]{:S(2)}) collective-permute-start(f32[4,22,8,256]{3,2,1,0:T(8,128)S(1)} %pad_maximum_fusion.mid), channel_id=1, source_target_pairs={{0,1},{1,0},{2,3},{3,2},{4,5},{5,4},{6,7},{7,6},{8,9},{9,8},{10,11... | collective-permute-start | bytes 2162696 | tf_op jit(solution)/shard_map/ppermute | solution.py:621
  23.9 0.0 collective-permute-done.3.odd
  23.9 1.8 %collective-permute-done.2.even = f32[4,22,8,256]{3,2,1,0:T(8,128)S(1)} collective-permute-done((f32[4,22,8,256]{3,2,1,0:T(8,128)S(1)}, f32[4,22,8,256]{3,2,1,0:T(8,128)S(1)}, u32[]{:S(2)}, u32[]{:S(2)}) %collective-permute-start.2) | collective-permute-done | bytes 720928 | tf_op jit(solution)/shard_map/ppermute | solution.py:621
  25.7 0.0 copy-done.3
  25.7 8.9 %setup.1 = (f32[6,20,24,256]{3,2,1,0:T(8,128)S(1)}, f32[3,20,24,256]{3,2,1,0:T(8,128)S(1)}, f32[3,20,24,256]{3,2,1,0:T(8,128)S(1)}, f32[20,24,256]{2,1,0:T(8,128...) custom-call(s32[2]{0:T(128)S(1)} %pad_add_fusion.where, ...), custom_call_target="tpu_custom_call" | custom-call | tf_op jit(solution)/shard_map/setup/pallas_call | solution.py:567
  34.7 19.2 %all_to_all.25.got.first = f32[32,1,512]{2,1,0:T(1,128)S(1)} all-to-all(f32[32,1,512]{2,1,0:T(1,128)S(1)} %get-tuple-element.40), channel_id=1, replica_groups=mesh['slab'=4,'block'=8] {'slab','block'}, dimensions={0} | all-to-all | bytes 131072 | tf_op jit(solution)/shard_map/all_to_all | solution.py:586
  53.8 17.0 %first.1 = (f32[3,8,8,256]{3,2,1,0:T(8,128)S(1)}, f32[3,16,16,256]{3,2,1,0:T(8,128)S(1)}, f32[32,1,128]{2,1,0:T(1,128)S(1)}) custom-call(s32[2]{0:T(128)S(1)} %pad_add_fusion.where, f32[79]{0:T(128)S(1)} %pad_maximum_fusion.2.coup, f32[32,1,512]{2,1,0:T(1,128)S(1)} %all_to_all.25.got.first, f32[6,20,24,256]{3,2,1,0:T(8,128)S(1)} %get-tuple-element.41.kh_w, ...), custom_call_target="tpu_custom_call" | custom-call | tf_op jit(solution)/shard_map/first/pallas_call | solution.py:567
  70.8 8.9 %all_to_all.26.got.got_old = f32[32,1,128]{2,1,0:T(1,128)S(1)} all-to-all(f32[32,1,128]{2,1,0:T(1,128)S(1)} %get-tuple-element.50), channel_id=1, replica_groups=mesh['slab'=4,'block'=8] {'slab','block'}, dimensions={0} | all-to-all | bytes 32768 | tf_op jit(solution)/shard_map/all_to_all | solution.py:586
  79.7 0.0 copy-start
  79.7 0.0 copy-start.2
  79.7 13.2 %second.1 = (f32[3,8,8,256]{3,2,1,0:T(8,128)S(1)}, f32[3,12,16,256]{3,2,1,0:T(8,128)S(1)}, f32[3,12,16,256]{3,2,1,0:T(8,128)S(1)}, f32[32,128]{1,0:T(8,128)S(1)}, f32[32,1,128]{2,1,0:T(1,128)S(1)}) custom-call(s32[2]{0:T(128)S(1)} %pad_add_fusion.where, f32[79]{0:T(128)S(1)} %pad_maximum_fusion.2.coup, f32[32,1,128]{2,1,0:T(1,128)S(1)} %all_to_all.26.got.got_old, ...), custom_call_target="tpu_custom_call" | custom-call | tf_op jit(solution)/shard_map/second/pallas_call | solution.py:567
  92.9 8.9 %all_to_all.27.got = f32[32,1,128]{2,1,0:T(1,128)S(1)} all-to-all(f32[32,1,128]{2,1,0:T(1,128)S(1)} %get-tuple-element.54), channel_id=1, replica_groups=mesh['slab'=4,'block'=8] {'slab','block'}, dimensions={0} | all-to-all | bytes 32768 | tf_op jit(solution)/shard_map/all_to_all | solution.py:586
  101.7 0.0 copy-done
  101.7 0.0 copy-done.2
  101.7 7.9 %third.1 = (f32[3,8,8,256]{3,2,1,0:T(8,128)S(1)}, f32[3,8,8,256]{3,2,1,0:T(8,128)S(1)}, f32[3,8,8,256]{3,2,1,0:T(8,128)S(1)}, f32[1,128]{1,0:T(1,128)S(1)}, f32[32,1,256]{2,1,0:T(1,128)S(1)}) custom-call(s32[2]{0:T(128)S(1)} %pad_add_fusion.where, f32[79]{0:T(128)S(1)} %pad_maximum_fusion.2.coup, f32[32,1,128]{2,1,0:T(1,128)S(1)} %all_to_all.27.got, ...), custom_call_target="tpu_custom_call" | custom-call | tf_op jit(solution)/shard_map/third/pallas_call | solution.py:567
  109.6 8.9 %all_to_all.28.got = f32[32,1,256]{2,1,0:T(1,128)S(1)} all-to-all(f32[32,1,256]{2,1,0:T(1,128)S(1)} %get-tuple-element.60), channel_id=1, replica_groups=mesh['slab'=4,'block'=8] {'slab','block'}, dimensions={0} | all-to-all | bytes 65536 | tf_op jit(solution)/shard_map/all_to_all | solution.py:586
  118.6 1.3 %last.1 = (f32[3,8,8,256]{3,2,1,0:T(8,128)}, f32[16]{0:T(128)}, f32[1]{0:T(128)}, f32[32,1,128]{2,1,0:T(1,128)S(1)}) custom-call(f32[32,1,256]{2,1,0:T(1,128)S(1)} %all_to_all.28.got, f32[1,128]{1,0:T(1,128)S(1)} %get-tuple-element.61.scal, f32[3,8,8,256]{3,2,1,0:T(8,128)S(1)} %get-tuple-element.62.base, f32[3,8,8,256]{3,2,1,0:T(8,128)S(1)} %get-tuple-element.63.z, ...), custom_call_target="tpu_custom_call" | custom-call | tf_op jit(solution)/shard_map/last/pallas_call | solution.py:567
  119.9 8.9 %all_to_all.29.got = f32[32,1,128]{2,1,0:T(1,128)S(1)} all-to-all(f32[32,1,128]{2,1,0:T(1,128)S(1)} %get-tuple-element.66), channel_id=1, replica_groups=mesh['slab'=4,'block'=8] {'slab','block'}, dimensions={0} | all-to-all | bytes 32768 | tf_op jit(solution)/shard_map/all_to_all | solution.py:586
  128.8 1.3 closing.1
  (5 shorter events, 0.1 us)
Async XLA Ops:
  0.6 19.5 %copy-start.1 = (f32[3,8,8,256]{3,2,1,0:T(8,128)S(1)}, f32[3,8,8,256]{3,2,1,0:T(8,128)}, u32[]{:S(2)}) copy-start(f32[3,8,8,256]{3,2,1,0:T(8,128)} %lanczos.3) | copy-start | bytes 589828
  2.4 23.4 %copy-start.3 = (f32[3,96]{1,0:T(4,128)S(1)}, f32[3,96]{1,0:T(4,128)}, u32[]{:S(2)}) copy-start(f32[3,96]{1,0:T(4,128)} %cinv) | copy-start | bytes 3460
  3.5 8.2 %collective-permute-start = (f32[4,7,8,256]{3,2,1,0:T(8,128)S(1)}, f32[4,7,8,256]{3,2,1,0:T(8,128)S(1)}, u32[]{:S(2)}, u32[]{:S(2)}) collective-permute-start(f32[4,7,8,256]{3,2,1,0:T(8,128)S(1)} %get-tuple-element.71), channel_id=1, source_target_pairs={{8,16},{16,8},{9,17},{17,9},{10,18},{18,10},{11,19},{19,11},{12,20... | collective-permute-start | bytes 688136 | tf_op jit(solution)/shard_map/ppermute | solution.py:615
  4.2 15.9 %collective-permute-start.1 = (f32[4,7,8,256]{3,2,1,0:T(8,128)S(1)}, f32[4,7,8,256]{3,2,1,0:T(8,128)S(1)}, u32[]{:S(2)}, u32[]{:S(2)}) collective-permute-start(f32[4,7,8,256]{3,2,1,0:T(8,128)S(1)} %get-tuple-element.72), channel_id=1, source_target_pairs={{0,8},{8,0},{16,24},{24,16},{1,9},{9,1},{17,25},{25,17},{2,10},{10... | collective-permute-start | bytes 688136 | tf_op jit(solution)/shard_map/ppermute | solution.py:614
  20.2 3.7 %collective-permute-start.3 = (f32[4,22,8,256]{3,2,1,0:T(8,128)S(1)}, f32[4,22,8,256]{3,2,1,0:T(8,128)S(1)}, u32[]{:S(2)}, u32[]{:S(2)}) collective-permute-start(f32[4,22,8,256]{3,2,1,0:T(8,128)S(1)} %pad_maximum_fusion.mid), channel_id=1, source_target_pairs={{1,2},{2,1},{3,4},{4,3},{5,6},{6,5},{9,10},{10,9},{11,12},{12,11},... | collective-permute-start | bytes 2162696 | tf_op jit(solution)/shard_map/ppermute | solution.py:622
  20.9 4.8 %collective-permute-start.2 = (f32[4,22,8,256]{3,2,1,0:T(8,128)S(1)}, f32[4,22,8,256]{3,2,1,0:T(8,128)S(1)}, u32[]{:S(2)}, u32[]{:S(2)}) collective-permute-start(f32[4,22,8,256]{3,2,1,0:T(8,128)S(1)} %pad_maximum_fusion.mid), channel_id=1, source_target_pairs={{0,1},{1,0},{2,3},{3,2},{4,5},{5,4},{6,7},{7,6},{8,9},{9,8},{10,11... | collective-permute-start | bytes 2162696 | tf_op jit(solution)/shard_map/ppermute | solution.py:621
  79.7 22.0 %copy-start = (f32[16,3,8,8,256]{4,3,2,1,0:T(8,128)S(1)}, f32[16,3,8,8,256]{4,3,2,1,0:T(8,128)}, u32[]{:S(2)}) copy-start(f32[16,3,8,8,256]{4,3,2,1,0:T(8,128)} %locked.3) | copy-start | bytes 9437188
  79.7 22.0 %copy-start.2 = (f32[3,8,8,256]{3,2,1,0:T(8,128)S(1)}, f32[3,8,8,256]{3,2,1,0:T(8,128)}, u32[]{:S(2)}) copy-start(f32[3,8,8,256]{3,2,1,0:T(8,128)} %previous.1) | copy-start | bytes 589828

commit v3 on v2

--- a/solution.py
+++ b/solution.py
@@ -19,14 +19,12 @@
 MID = (4, 16)
 OWN = (0, 8)
 REACH = 2 * ITERS
-PAIRS = [(n // 9 - 1, n // 3 % 3 - 1, n % 3 - 1) for n in range(13)]
+HALF = [(-1, -1), (-1, 0), (-1, 1), (0, -1)]
 f32 = jnp.float32
 
 
-def along_z(field, dz):
-    rows, depth = field.shape
-    lane = lax.broadcasted_iota(jnp.int32, (rows, LANES), 1)
-    chunks = [field[:, low : low + LANES] for low in range(0, depth, LANES)]
+def along_z(chunks, dz):
+    lane = lax.broadcasted_iota(jnp.int32, chunks[0].shape, 1)
     turned = [pltpu.roll(chunk, (-dz) % LANES, 1) for chunk in chunks]
     edge = 0 if dz < 0 else LANES - 1
     out = []
@@ -34,7 +32,7 @@
         other = number + dz
         filler = turned[other] if 0 <= other < len(turned) else 0.0
         out.append(jnp.where(lane == edge, filler, chunk))
-    return jnp.concatenate(out, axis=1)
+    return out
 
 
 def shift_store(dest, at, fields, source, target):
@@ -46,30 +44,45 @@
             moved = field if shift == 0 else pltpu.roll(field, (-shift) % src_rows, 0)
             if dst_rows != src_rows:
                 moved = moved[:dst_rows]
-            for dz in (-1, 0, 1):
-                out = moved if dz == 0 else along_z(moved, dz)
-                dest[((dy + 1) * 3 + dz + 1) * len(fields) + comp, at] = out
-
-
-def pair_slots(pair):
-    dx, dy, dz = pair
-    return dx, (dy + 1) * 3 + dz + 1, (1 - dy) * 3 + 1 - dz
+            dest[(dy + 1) * len(fields) + comp, at] = moved
+
+
+def gather_z(parts):
+    flat, up, down = zip(*parts)
+    above, below = along_z(up, 1), along_z(down, -1)
+    return jnp.concatenate([a + (b + c) for a, b, c in zip(flat, above, below)], axis=1)
 
 
 def stencil(moved, at, coup, center):
-    near = [moved[4 * 3 + c, at] for c in range(3)]
-    total = [center(i) * value for i, value in enumerate(six_of(near))]
-    for number, pair in enumerate(PAIRS):
-        dx, plus, minus = pair_slots(pair)
-        sums = [moved[plus * 3 + c, at + dx] + moved[minus * 3 + c, at - dx] for c in range(3)]
-        for i, value in enumerate(six_of(sums)):
-            total[i] = total[i] + coup[number * 6 + i] * value
-    out = [
-        total[0] + (total[3] + total[4]),
-        total[1] + (total[3] + total[5]),
-        total[2] + (total[4] + total[5]),
-    ]
-    return out, near
+    depth = moved.shape[3]
+    parts = [[], [], []]
+    rows = []
+    for low in range(0, depth, LANES):
+        cut = slice(low, low + LANES)
+        near = [moved[3 + c, at, :, cut] for c in range(3)]
+        rows.append(near)
+        flat, up, down = [], [], [None] * 6
+        for i, value in enumerate(six_of(near)):
+            flat.append(center(i, cut) * value)
+            up.append(coup[18 * len(HALF) + i] * value)
+        for q, (dx, dy) in enumerate(HALF):
+            plus = [moved[(dy + 1) * 3 + c, at + dx, :, cut] for c in range(3)]
+            minus = [moved[(1 - dy) * 3 + c, at - dx, :, cut] for c in range(3)]
+            for i, value in enumerate(six_of([p + m for p, m in zip(plus, minus)])):
+                flat[i] = flat[i] + coup[q * 18 + i] * value
+                up[i] = up[i] + coup[q * 18 + 6 + i] * value
+            for i, value in enumerate(six_of([p - m for p, m in zip(plus, minus)])):
+                term = coup[q * 18 + 12 + i] * value
+                down[i] = term if down[i] is None else down[i] + term
+        flat, up, down = fold(flat), fold(up), fold(down)
+        for k in range(3):
+            parts[k].append((flat[k], up[k] + down[k], up[k] - down[k]))
+    near = [jnp.concatenate([row[k] for row in rows], axis=1) for k in range(3)]
+    return [gather_z(one) for one in parts], near
+
+
+def fold(six):
+    return [six[0] + (six[3] + six[4]), six[1] + (six[3] + six[5]), six[2] + (six[4] + six[5])]
 
 
 def six_of(three):
@@ -151,22 +164,29 @@
 
 
 def center_row(moved_root, at, root, coup):
-    total = [None] * 6
-    for number, pair in enumerate(PAIRS):
-        dx, plus, minus = pair_slots(pair)
-        both = moved_root[plus, at + dx] + moved_root[minus, at - dx]
+    depth = root.shape[1]
+    parts = [[] for _ in range(6)]
+    for low in range(0, depth, LANES):
+        cut = slice(low, low + LANES)
+        flat, down = [None] * 6, [None] * 6
+        near = moved_root[1, at, :, cut]
+        up = [coup[18 * len(HALF) + i] * near for i in range(6)]
+        for q, (dx, dy) in enumerate(HALF):
+            plus, minus = moved_root[dy + 1, at + dx, :, cut], moved_root[1 - dy, at - dx, :, cut]
+            both, change = plus + minus, plus - minus
+            for i in range(6):
+                first, last = coup[q * 18 + i] * both, coup[q * 18 + 12 + i] * change
+                flat[i] = first if flat[i] is None else flat[i] + first
+                up[i] = up[i] + coup[q * 18 + 6 + i] * both
+                down[i] = last if down[i] is None else down[i] + last
         for i in range(6):
-            term = coup[number * 6 + i] * both
-            total[i] = term if total[i] is None else total[i] + term
+            parts[i].append((flat[i], up[i] + down[i], up[i] - down[i]))
+    total = [gather_z(one) for one in parts]
     inside = root > 0.0
     inverse = jnp.where(inside, 1.0 / jnp.where(inside, root, 1.0), 0.0)
     center = [-total[i] * inverse for i in range(6)]
     center[:3] = [one + SHIFT_MASS for one in center[:3]]
-    whole = [
-        center[0] + (center[3] + center[4]),
-        center[1] + (center[3] + center[5]),
-        center[2] + (center[4] + center[5]),
-    ]
+    whole = fold(center)
     half = [jnp.where(inside, SMOOTH_WEIGHT / one, 0.0) for one in whole]
     return center, half, inverse
 
@@ -235,7 +255,7 @@
 
     def remain(x, carry):
         for i in (2 * x, 2 * x + 1):
-            image, _ = stencil(moved_own, i + 1, coup, lambda slot: kh_o[slot, i])
+            image, _ = stencil(moved_own, i + 1, coup, lambda slot, cut: kh_o[slot, i, :, cut])
             carry = tuple(carry[k] + root_o[i] * (v_o[k, i] - image[k]) for k in range(3))
         return carry
 
@@ -295,7 +315,7 @@
 
     def body(x, carry):
         for i in (2 * x, 2 * x + 1):
-            image, _ = stencil(moved_own, i + 1, coup, lambda slot: center(slot, i))
+            image, _ = stencil(moved_own, i + 1, coup, lambda slot, cut: center(slot, i, cut))
             carry = tuple(carry[k] + root(i) * (own_of(mapped(k, i + 1)) - image[k]) for k in range(3))
         return carry
 
@@ -319,20 +339,20 @@
     )
 
     def image(x):
-        out, _ = stencil(moved_next, x + 1, coup, lambda i: kh_m[i, x])
+        out, _ = stencil(moved_next, x + 1, coup, lambda i, cut: kh_m[i, x, :, cut])
         for k in range(3):
             mapped[k, x] = out[k]
 
     iterate(
         (span, depth), level, (WIDE, WIDE, MID), coup, store,
         lambda k, x: v_w[k, x], lambda k, x: h_w[k, x], lambda x: root_w[x],
-        (lambda at: lambda i: kh_w[i, at]), moved, moved_next, z_all, image,
+        (lambda at: lambda i, cut: kh_w[i, at, :, cut]), moved, moved_next, z_all, image,
     )
     inner = level - 2
     parts = means_of(
         (span, depth), coup, lambda x: root_o[x],
         lambda k, x: h_m[k, x + 3], lambda k, x: mapped[k, x + inner - 1],
-        lambda i, x: kh_o[i, x], moved_own,
+        lambda i, x, cut: kh_o[i, x, :, cut], moved_own,
     )
 
     def dots(x, carry):
@@ -379,20 +399,20 @@
         return v_m[k, x] - size * mapped_old[k, x]
 
     def image(x):
-        out, _ = stencil(moved_next, x + 1, coup, lambda i: kh_m[i, x + 2])
+        out, _ = stencil(moved_next, x + 1, coup, lambda i, cut: kh_m[i, x + 2, :, cut])
         for k in range(3):
             mapped[k, x] = out[k]
 
     iterate(
         (span, depth), level, (MID, MID, MID), coup, store,
         rest, lambda k, x: h_m[k, x], lambda x: root_m[x],
-        (lambda at: lambda i: kh_m[i, at]), moved, moved_next, z_all, image,
+        (lambda at: lambda i, cut: kh_m[i, at, :, cut]), moved, moved_next, z_all, image,
     )
     inner = level - 2
     parts = means_of(
         (span, depth), coup, lambda x: root_o[x],
         lambda k, x: h_m[k, x + 3], lambda k, x: mapped[k, x + inner - 1],
-        lambda i, x: kh_o[i, x], moved_own,
+        lambda i, x, cut: kh_o[i, x, :, cut], moved_own,
     )
 
     def dots(x, carry):
@@ -458,12 +478,12 @@
     iterate(
         (span, depth), level, (MID, MID, OWN), coup, store,
         lambda k, x: residual[k, x], lambda k, x: h_m[k, x + 2], lambda x: root_m[x + 2],
-        (lambda at: lambda i: kh_m[i, at + 2]), moved, moved_next, z_all, None,
+        (lambda at: lambda i, cut: kh_m[i, at + 2, :, cut]), moved, moved_next, z_all, None,
     )
 
     def finish(x, carry):
         gamma, delta, cross, with_base, with_z, with_dir, weight = carry
-        image, near = stencil(moved_next, x + 1, coup, lambda i: kh_o[i, x])
+        image, near = stencil(moved_next, x + 1, coup, lambda i, cut: kh_o[i, x, :, cut])
         inverse = 1.0 / root_o[x]
         for k in range(3):
             z = near[k]
@@ -479,7 +499,7 @@
             weight = weight + lanczos[k, x] * lanczos[k, x]
             z_out[k, x] = z * inverse
             dir_out[k, x] = direction * inverse
-            base[k, x] = partial * inverse - coup[6 * len(PAIRS)] * previous[k, x]
+            base[k, x] = partial * inverse - coup[18 * len(HALF) + 6] * previous[k, x]
         return gamma, delta, cross, with_base, with_z, with_dir, weight
 
     zero = jnp.zeros((8, depth), f32)
@@ -600,7 +620,9 @@
     flat = -couplings.reshape(-1, 9)
     a, b, c = flat[:, 1], flat[:, 2], flat[:, 5]
     six = jnp.stack([flat[:, 0] - a - b, flat[:, 4] - a - c, flat[:, 8] - b - c, a, b, c], axis=1)
-    coup = jnp.concatenate([six.reshape(-1), previous_beta.reshape(1)])
+    flat, up, down = six[1:12:3], six[2:12:3], six[0:12:3]
+    groups = jnp.stack([flat, 0.5 * (up + down), 0.5 * (up - down)], axis=1)
+    coup = jnp.concatenate([groups.reshape(-1), six[12], previous_beta.reshape(1)])
 
     density = jnp.where(occupancy == 1, 1.0, VOID_DENSITY).astype(f32)
     density = jnp.repeat(jnp.repeat(jnp.repeat(density, BRICK, 0), BRICK, 1), BRICK, 2)
@@ -639,9 +661,9 @@
             (6, *own[1:]), own, own[1:], (devices, 1, LANES + 3 * padded),
         ],
         [
-            scratch(9, span + 2 * halo + 1, WIDE[1], depth),
+            scratch(3, span + 2 * halo + 1, WIDE[1], depth),
             scratch(span + 2 * halo + 1, WIDE[1], depth),
-            scratch(27, span + 2, 8, depth),
+            scratch(9, span + 2, 8, depth),
             scratch(8, depth),
         ],
         where, coup, side_near, side_far, tall, coarse_inverse, limit=9 << 20,
@@ -654,9 +676,9 @@
         "first",
         [own, (3, *mid), row],
         [
-            scratch(27, *wide),
-            scratch(27, span + 2 * REACH - 2, MID[1], depth),
-            scratch(27, span + 2, 8, depth),
+            scratch(9, *wide),
+            scratch(9, span + 2 * REACH - 2, MID[1], depth),
+            scratch(9, span + 2, 8, depth),
             scratch(3, span + 2 * REACH - 2, WIDE[1], depth),
             store,
             scratch(8, depth),
@@ -672,9 +694,9 @@
         "second",
         [own, inner, inner, (devices, LANES), row],
         [
-            scratch(27, *mid),
-            scratch(27, span + 2 * level - 2, MID[1], depth),
-            scratch(27, span + 2, 8, depth),
+            scratch(9, *mid),
+            scratch(9, span + 2 * level - 2, MID[1], depth),
+            scratch(9, span + 2, 8, depth),
             scratch(3, span + 2 * level - 2, MID[1], depth),
             store,
             scratch(8, depth),
@@ -689,8 +711,8 @@
         "third",
         [own, own, own, (1, LANES), (devices, 1, 2 * LANES)],
         [
-            scratch(27, span + 2 * level, MID[1], depth),
-            scratch(27, span + 2 * level - 2, 8, depth),
+            scratch(9, span + 2 * level, MID[1], depth),
+            scratch(9, span + 2 * level - 2, 8, depth),
             scratch(3, span + 2 * level, MID[1], depth),
             scratch(3, span + 2 * level, MID[1], depth),
             scratch(3, span + 2 * level - 2, MID[1], depth),

time: 130 us -> 113 us (0.87)
  Pallas kernels: 49.6 us -> 32 us
    pallas_call x6, Pallas kernels: 49.6 us -> 32 us  [call(): pl.pallas_call(kernel, name=name, out_shape=[jax.ShapeDtypeStruct(shape,...]
  transfers between devices with their start and end apart: 4 -> 4, of which waited for: 2 -> 2; matrix products, arithmetic and copies ran while one was open for 1% -> 2% of each run, Pallas kernels for 0% -> 0%
where the time goes in v3:
time: 113 us; the launch traced here: 112 us
  blocking collectives  54.7 us (48%)
  Pallas kernels  32 us (28%)
  starting transfers between devices  10.1 us (9%)
  waiting for transfers between devices  9.57 us (8%)
  other arithmetic  3.67 us (3%)
  between operations  1.41 us (1%)
    all_to_all x5, blocking collectives, exchange_rows(): return lax.all_to_all(rows, AXES, 0, 0, tiled=True)  54.7 us
    pallas_call x6, Pallas kernels, call(): pl.pallas_call(kernel, name=name, out_shape=[jax.ShapeDtypeStruct(shape,...  32 us
    ppermute x1, waiting for transfers between devices, shards(): from_near = lax.ppermute(jnp.where(odd == 0, upper, lower), 'slab', near)  7.75 us
    ppermute x1, starting transfers between devices, shards(): from_near = lax.ppermute(jnp.where(odd == 0, upper, lower), 'slab', near)  5.76 us
    ppermute x1, starting transfers between devices, shards(): side_near = lax.ppermute(tall, 'block', near)  2.96 us
  transfers between devices with their start and end apart: 4, of which 2 were waited for; matrix products, arithmetic and copies ran while one was open for 2% of the time, Pallas kernels for 0%

profile of v3, /device:TPU:0, one launch (start us, length us, event | category | flops | bytes accessed | tf_op | source)
XLA Modules:
  0.0 112.5 jit_solution(7420115397443937599)
XLA Ops:
  0.6 0.0 copy-start.1
  0.7 0.7 fusion.3
  1.4 0.1 broadcast_in_dim.22
  1.4 0.1 broadcast_in_dim.23
  1.5 0.9 multiply_bitcast_fusion
  2.4 0.0 copy-start.3
  2.4 1.2 %fusion.1 = (f32[4,7,8,256]{3,2,1,0:T(8,128)S(1)}, f32[4,7,8,256]{3,2,1,0:T(8,128)S(1)}) fusion(f32[1,8,8,256]{3,2,1,0:T(8,128)S(1)} %multiply_bitcast_fusion, f32[3,8,8,256]{3,2,1,0:T(8,128)} %lanczos.3, pred[]{:T(512)S(6)} %eq.14), kind=kLoop, calls=%fused_computation.5 | loop fusion | flops 286720 | bytes 720897 | tf_op jit(solution)/shard_map/jit(_where)/select_n | solution.py:637
  3.5 0.7 collective-permute-start
  4.2 5.8 %collective-permute-start.1 = (f32[4,7,8,256]{3,2,1,0:T(8,128)S(1)}, f32[4,7,8,256]{3,2,1,0:T(8,128)S(1)}, u32[]{:S(2)}, u32[]{:S(2)}) collective-permute-start(f32[4,7,8,256]{3,2,1,0:T(8,128)S(1)} %get-tuple-element.72), channel_id=1, source_target_pairs={{0,8},{8,0},{16,24},{24,16},{1,9},{9,1},{17,25},{25,17},{2,10},{10... | collective-permute-start | bytes 688136 | tf_op jit(solution)/shard_map/ppermute | solution.py:636
  10.0 0.7 neg.6
  10.7 0.1 slice.50
  10.8 0.1 slice.49
  10.9 0.1 slice.48
  11.0 0.1 copy.15
  11.1 0.1 copy.16
  11.2 0.1 copy.17
  11.3 0.1 pad_add_fusion.where
  12.0 0.1 reshape.19
  12.1 0.2 slice_reduce_fusion
  12.3 0.1 pad_maximum_fusion.3.coup
  12.4 0.0 collective-permute-done
  12.4 7.8 %collective-permute-done.1 = f32[4,7,8,256]{3,2,1,0:T(8,128)S(1)} collective-permute-done((f32[4,7,8,256]{3,2,1,0:T(8,128)S(1)}, f32[4,7,8,256]{3,2,1,0:T(8,128)S(1)}, u32[]{:S(2)}, u32[]{:S(2)}) %collective-permute-start.1) | collective-permute-done | bytes 229408 | tf_op jit(solution)/shard_map/ppermute | solution.py:636
  20.2 0.0 copy-done.1
  20.2 0.1 pad_maximum_fusion.mid
  20.2 0.7 collective-permute-start.3
  21.0 3.0 %collective-permute-start.2 = (f32[4,22,8,256]{3,2,1,0:T(8,128)S(1)}, f32[4,22,8,256]{3,2,1,0:T(8,128)S(1)}, u32[]{:S(2)}, u32[]{:S(2)}) collective-permute-start(f32[4,22,8,256]{3,2,1,0:T(8,128)S(1)} %pad_maximum_fusion.mid), channel_id=1, source_target_pairs={{0,1},{1,0},{2,3},{3,2},{4,5},{5,4},{6,7},{7,6},{8,9},{9,8},{10,11... | collective-permute-start | bytes 2162696 | tf_op jit(solution)/shard_map/ppermute | solution.py:643
  23.9 0.0 collective-permute-done.3.odd
  23.9 1.8 %collective-permute-done.2.even = f32[4,22,8,256]{3,2,1,0:T(8,128)S(1)} collective-permute-done((f32[4,22,8,256]{3,2,1,0:T(8,128)S(1)}, f32[4,22,8,256]{3,2,1,0:T(8,128)S(1)}, u32[]{:S(2)}, u32[]{:S(2)}) %collective-permute-start.2) | collective-permute-done | bytes 720928 | tf_op jit(solution)/shard_map/ppermute | solution.py:643
  25.7 0.0 copy-done.3
  25.7 6.2 %setup.1 = (f32[6,20,24,256]{3,2,1,0:T(8,128)S(1)}, f32[3,20,24,256]{3,2,1,0:T(8,128)S(1)}, f32[3,20,24,256]{3,2,1,0:T(8,128)S(1)}, f32[20,24,256]{2,1,0:T(8,128...) custom-call(s32[2]{0:T(128)S(1)} %pad_add_fusion.where, ...), custom_call_target="tpu_custom_call" | custom-call | tf_op jit(solution)/shard_map/setup/pallas_call | solution.py:587
  32.0 19.2 %all_to_all.25.got.first = f32[32,1,512]{2,1,0:T(1,128)S(1)} all-to-all(f32[32,1,512]{2,1,0:T(1,128)S(1)} %get-tuple-element.40), channel_id=1, replica_groups=mesh['slab'=4,'block'=8] {'slab','block'}, dimensions={0} | all-to-all | bytes 131072 | tf_op jit(solution)/shard_map/all_to_all | solution.py:606
  51.1 9.7 %first.1 = (f32[3,8,8,256]{3,2,1,0:T(8,128)S(1)}, f32[3,16,16,256]{3,2,1,0:T(8,128)S(1)}, f32[32,1,128]{2,1,0:T(1,128)S(1)}) custom-call(s32[2]{0:T(128)S(1)} %pad_add_fusion.where, f32[79]{0:T(128)S(1)} %pad_maximum_fusion.3.coup, f32[32,1,512]{2,1,0:T(1,128)S(1)} %all_to_all.25.got.first, f32[6,20,24,256]{3,2,1,0:T(8,128)S(1)} %get-tuple-element.41.kh_w, ...), custom_call_target="tpu_custom_call" | custom-call | tf_op jit(solution)/shard_map/first/pallas_call | solution.py:587
  60.8 8.9 %all_to_all.26.got.got_old = f32[32,1,128]{2,1,0:T(1,128)S(1)} all-to-all(f32[32,1,128]{2,1,0:T(1,128)S(1)} %get-tuple-element.50), channel_id=1, replica_groups=mesh['slab'=4,'block'=8] {'slab','block'}, dimensions={0} | all-to-all | bytes 32768 | tf_op jit(solution)/shard_map/all_to_all | solution.py:606
  69.7 0.0 copy-start
  69.7 0.0 copy-start.2
  69.7 7.5 %second.1 = (f32[3,8,8,256]{3,2,1,0:T(8,128)S(1)}, f32[3,12,16,256]{3,2,1,0:T(8,128)S(1)}, f32[3,12,16,256]{3,2,1,0:T(8,128)S(1)}, f32[32,128]{1,0:T(8,128)S(1)}, f32[32,1,128]{2,1,0:T(1,128)S(1)}) custom-call(s32[2]{0:T(128)S(1)} %pad_add_fusion.where, f32[79]{0:T(128)S(1)} %pad_maximum_fusion.3.coup, f32[32,1,128]{2,1,0:T(1,128)S(1)} %all_to_all.26.got.got_old, ...), custom_call_target="tpu_custom_call" | custom-call | tf_op jit(solution)/shard_map/second/pallas_call | solution.py:587
  77.2 8.9 %all_to_all.27.got = f32[32,1,128]{2,1,0:T(1,128)S(1)} all-to-all(f32[32,1,128]{2,1,0:T(1,128)S(1)} %get-tuple-element.54), channel_id=1, replica_groups=mesh['slab'=4,'block'=8] {'slab','block'}, dimensions={0} | all-to-all | bytes 32768 | tf_op jit(solution)/shard_map/all_to_all | solution.py:606
  86.0 0.0 copy-done
  86.0 0.0 copy-done.2
  86.0 6.0 %third.1 = (f32[3,8,8,256]{3,2,1,0:T(8,128)S(1)}, f32[3,8,8,256]{3,2,1,0:T(8,128)S(1)}, f32[3,8,8,256]{3,2,1,0:T(8,128)S(1)}, f32[1,128]{1,0:T(1,128)S(1)}, f32[32,1,256]{2,1,0:T(1,128)S(1)}) custom-call(s32[2]{0:T(128)S(1)} %pad_add_fusion.where, f32[79]{0:T(128)S(1)} %pad_maximum_fusion.3.coup, f32[32,1,128]{2,1,0:T(1,128)S(1)} %all_to_all.27.got, ...), custom_call_target="tpu_custom_call" | custom-call | tf_op jit(solution)/shard_map/third/pallas_call | solution.py:587
  92.0 8.9 %all_to_all.28.got = f32[32,1,256]{2,1,0:T(1,128)S(1)} all-to-all(f32[32,1,256]{2,1,0:T(1,128)S(1)} %get-tuple-element.60), channel_id=1, replica_groups=mesh['slab'=4,'block'=8] {'slab','block'}, dimensions={0} | all-to-all | bytes 65536 | tf_op jit(solution)/shard_map/all_to_all | solution.py:606
  101.0 1.3 %last.1 = (f32[3,8,8,256]{3,2,1,0:T(8,128)}, f32[16]{0:T(128)}, f32[1]{0:T(128)}, f32[32,1,128]{2,1,0:T(1,128)S(1)}) custom-call(f32[32,1,256]{2,1,0:T(1,128)S(1)} %all_to_all.28.got, f32[1,128]{1,0:T(1,128)S(1)} %get-tuple-element.61.scal, f32[3,8,8,256]{3,2,1,0:T(8,128)S(1)} %get-tuple-element.62.base, f32[3,8,8,256]{3,2,1,0:T(8,128)S(1)} %get-tuple-element.63.z, ...), custom_call_target="tpu_custom_call" | custom-call | tf_op jit(solution)/shard_map/last/pallas_call | solution.py:587
  102.3 8.9 %all_to_all.29.got = f32[32,1,128]{2,1,0:T(1,128)S(1)} all-to-all(f32[32,1,128]{2,1,0:T(1,128)S(1)} %get-tuple-element.66), channel_id=1, replica_groups=mesh['slab'=4,'block'=8] {'slab','block'}, dimensions={0} | all-to-all | bytes 32768 | tf_op jit(solution)/shard_map/all_to_all | solution.py:606
  111.2 1.3 %closing.1 = f32[2]{0:T(128)} custom-call(f32[32,1,128]{2,1,0:T(1,128)S(1)} %all_to_all.29.got, f32[1]{0:T(128)} %get-tuple-element.67.found), custom_call_target="tpu_custom_call" | custom-call | tf_op jit(solution)/shard_map/closing/pallas_call | solution.py:587
  (8 shorter events, 0.1 us)
Async XLA Ops:
  0.6 19.5 %copy-start.1 = (f32[3,8,8,256]{3,2,1,0:T(8,128)S(1)}, f32[3,8,8,256]{3,2,1,0:T(8,128)}, u32[]{:S(2)}) copy-start(f32[3,8,8,256]{3,2,1,0:T(8,128)} %lanczos.3) | copy-start | bytes 589828
  2.4 23.4 %copy-start.3 = (f32[3,96]{1,0:T(4,128)S(1)}, f32[3,96]{1,0:T(4,128)}, u32[]{:S(2)}) copy-start(f32[3,96]{1,0:T(4,128)} %cinv) | copy-start | bytes 3460
  3.5 8.8 %collective-permute-start = (f32[4,7,8,256]{3,2,1,0:T(8,128)S(1)}, f32[4,7,8,256]{3,2,1,0:T(8,128)S(1)}, u32[]{:S(2)}, u32[]{:S(2)}) collective-permute-start(f32[4,7,8,256]{3,2,1,0:T(8,128)S(1)} %get-tuple-element.71), channel_id=1, source_target_pairs={{8,16},{16,8},{9,17},{17,9},{10,18},{18,10},{11,19},{19,11},{12,20... | collective-permute-start | bytes 688136 | tf_op jit(solution)/shard_map/ppermute | solution.py:637
  4.2 15.9 %collective-permute-start.1 = (f32[4,7,8,256]{3,2,1,0:T(8,128)S(1)}, f32[4,7,8,256]{3,2,1,0:T(8,128)S(1)}, u32[]{:S(2)}, u32[]{:S(2)}) collective-permute-start(f32[4,7,8,256]{3,2,1,0:T(8,128)S(1)} %get-tuple-element.72), channel_id=1, source_target_pairs={{0,8},{8,0},{16,24},{24,16},{1,9},{9,1},{17,25},{25,17},{2,10},{10... | collective-permute-start | bytes 688136 | tf_op jit(solution)/shard_map/ppermute | solution.py:636
  20.2 3.7 %collective-permute-start.3 = (f32[4,22,8,256]{3,2,1,0:T(8,128)S(1)}, f32[4,22,8,256]{3,2,1,0:T(8,128)S(1)}, u32[]{:S(2)}, u32[]{:S(2)}) collective-permute-start(f32[4,22,8,256]{3,2,1,0:T(8,128)S(1)} %pad_maximum_fusion.mid), channel_id=1, source_target_pairs={{1,2},{2,1},{3,4},{4,3},{5,6},{6,5},{9,10},{10,9},{11,12},{12,11},... | collective-permute-start | bytes 2162696 | tf_op jit(solution)/shard_map/ppermute | solution.py:644
  21.0 4.8 %collective-permute-start.2 = (f32[4,22,8,256]{3,2,1,0:T(8,128)S(1)}, f32[4,22,8,256]{3,2,1,0:T(8,128)S(1)}, u32[]{:S(2)}, u32[]{:S(2)}) collective-permute-start(f32[4,22,8,256]{3,2,1,0:T(8,128)S(1)} %pad_maximum_fusion.mid), channel_id=1, source_target_pairs={{0,1},{1,0},{2,3},{3,2},{4,5},{5,4},{6,7},{7,6},{8,9},{9,8},{10,11... | collective-permute-start | bytes 2162696 | tf_op jit(solution)/shard_map/ppermute | solution.py:643
  69.7 16.3 %copy-start = (f32[16,3,8,8,256]{4,3,2,1,0:T(8,128)S(1)}, f32[16,3,8,8,256]{4,3,2,1,0:T(8,128)}, u32[]{:S(2)}) copy-start(f32[16,3,8,8,256]{4,3,2,1,0:T(8,128)} %locked.3) | copy-start | bytes 9437188
  69.7 16.3 %copy-start.2 = (f32[3,8,8,256]{3,2,1,0:T(8,128)S(1)}, f32[3,8,8,256]{3,2,1,0:T(8,128)}, u32[]{:S(2)}) copy-start(f32[3,8,8,256]{3,2,1,0:T(8,128)} %previous.1) | copy-start | bytes 589828

commit v4 on v3

--- a/solution.py
+++ b/solution.py
@@ -118,16 +118,16 @@
     return one[0, 0]
 
 
-def coarse_values(means, rows_of, where, counts, store):
-    total = None
+def coarse_values(means, rows, store):
+    shape = (means.shape[0], rows.shape[1])
+    row = lax.broadcasted_iota(jnp.int32, shape, 0)
+    lane = lax.broadcasted_iota(jnp.int32, shape, 1)
+    spread = jnp.zeros(shape, f32)
     for k in range(3):
-        part = row_sum(rows_of(k) * means[:, k : k + 1])
-        total = part if total is None else total + part
-    for bx in range(3):
-        for by in range(3):
-            spot = (where[0] + bx - 1) * counts[1] + where[1] + by - 1
-            for k in range(3):
-                store[(bx * 3 + by) * 3 + k] = scalar(pick(total, spot * 3 + k))
+        spread = jnp.where(lane == 3 * row + k, means[:, k : k + 1], spread)
+    column = jnp.sum(rows[...] * row_sum(spread), axis=1, keepdims=True)
+    for slot in range(27):
+        store[slot] = column[slot, 0]
 
 
 def correction(store, x, k, layout, span, depth):
@@ -143,16 +143,82 @@
     msg[:, :, low : low + width] = jnp.broadcast_to(row.reshape(1, 1, width), (count, 1, width))
 
 
-def side_rows(where, even, odd, mid):
+def pack_kernel(
+    dims, where, occupancy, vector_in, young_in, cinv_in,
+    near, far, vector, stiff, coarse,
+    young, cinv, sems,
+):
+    span, depth, _ = dims
+    copies = [
+        pltpu.make_async_copy(source, target, sems.at[number])
+        for number, (source, target) in enumerate([(young_in, young), (cinv_in, cinv), (vector_in, vector)])
+    ]
+    for copy in copies:
+        copy.start()
+    lane = lax.broadcasted_iota(jnp.int32, (8, depth), 1)
+    density = jnp.full((8, depth), VOID_DENSITY, f32)
+    for brick in range(depth // BRICK):
+        solid = jnp.where(occupancy[brick] == 1, 1.0, VOID_DENSITY).astype(f32)
+        density = jnp.where(lane // BRICK == brick, solid, density)
+    for copy in copies:
+        copy.wait()
+    for x in range(span):
+        stiff[x] = density * young[x]
+    width = cinv.shape[1]
+    coarse[...] = jnp.zeros_like(coarse)
+    for t in range(coarse.shape[0]):
+        count = min(depth, width - t * depth)
+        coarse[t, 0:3, 0:count] = cinv[:, t * depth : t * depth + count]
+    flip = where[0] % 2 == 1
+    halo = REACH + 1
+
+    def put(tile, low, high):
+        near[tile] = jnp.where(flip, low, high)
+        far[tile] = jnp.where(flip, high, low)
+
+    for k in range(3):
+        for j in range(REACH):
+            put(k * REACH + j, vector[k, j], vector[k, span - REACH + j])
+    for j in range(halo):
+        put(3 * REACH + j, stiff[j], stiff[span - halo + j])
+    for t in range(coarse.shape[0]):
+        put(3 * REACH + halo + t, coarse[t], coarse[t])
+
+
+def tall_kernel(dims, where, near, far, vector, stiff, coarse, tall):
+    span, _, _ = dims
+    halo = REACH + 1
+    flip = where[0] % 2 == 1
+
+    def sides(tile):
+        first, second = near[tile], far[tile]
+        return jnp.where(flip, first, second), jnp.where(flip, second, first)
+
+    for k in range(3):
+        base = k * (span + 2 * REACH)
+        for j in range(REACH):
+            tall[base + j], tall[base + REACH + span + j] = sides(k * REACH + j)
+        for x in range(span):
+            tall[base + REACH + x] = vector[k, x]
+    base = 3 * (span + 2 * REACH)
+    for j in range(halo):
+        tall[base + j], tall[base + halo + span + j] = sides(3 * REACH + j)
+    for x in range(span):
+        tall[base + halo + x] = stiff[x]
+    base, pieces = base + span + 2 * halo, coarse.shape[0]
+    for t in range(pieces):
+        tall[base + t], tall[base + 2 * pieces + t] = sides(3 * REACH + halo + t)
+        tall[base + pieces + t] = coarse[t]
+
+
+def side_tiles(where, even, odd, mid):
     flip = where[1] % 2 == 1
 
-    def wide(comp, x):
-        first, second = even[comp, x], odd[comp, x]
-        low = jnp.where(flip, first, second)
-        high = jnp.where(flip, second, first)
-        return jnp.concatenate([low, mid[comp, x], high], axis=0)
-
-    return wide
+    def three(tile):
+        first, second = even[tile], odd[tile]
+        return jnp.where(flip, first, second), mid[tile], jnp.where(flip, second, first)
+
+    return three
 
 
 def repack(field):
@@ -192,16 +258,21 @@
 
 
 def setup_kernel(
-    dims, where, coup, even, odd, mid, cinv,
-    kh_w, h_w, v_w, root_w, kh_m, h_m, v_m, root_m, kh_o, v_o, root_o, msg,
+    dims, where, coup, even, odd, mid,
+    kh_w, h_w, v_w, root_w, kh_m, h_m, v_m, root_m, kh_o, v_o, root_o, coarse_rows, msg,
     moved_root, root_all, moved_own, sums,
 ):
     span, depth, devices = dims
     halo = REACH + 1
-    wide = side_rows(where, even, odd, mid)
+    three = side_tiles(where, even, odd, mid)
+    count = span + 2 * REACH
+
+    def wide(tile):
+        return jnp.concatenate(three(tile), axis=0)
+
 
     def roots(x):
-        root = jnp.sqrt(wide(3, x))
+        root = jnp.sqrt(wide(3 * count + x))
         root_all[x] = root
         shift_store(moved_root, x, [root], WIDE, WIDE)
 
@@ -210,7 +281,7 @@
         root = root_all[at]
         center, half, inverse = center_row(moved_root, at, root, coup)
         m, o = x - (REACH - 4), x - REACH
-        vectors = [wide(k, at) * inverse for k in range(3)]
+        vectors = [wide(k * count + x) * inverse for k in range(3)]
         root_w[x] = root
         for k in range(3):
             h_w[k, x] = half[k]
@@ -265,13 +336,14 @@
     for k in range(3):
         sums[k : k + 1] = row_sum(parts[k])
     send(msg, 0, to_lanes(sums[...]) * (1.0 / (span * 8 * depth)), devices)
-    width = cinv.shape[1]
-    padded = (msg.shape[2] - LANES) // 3
-    for k in range(3):
-        row = cinv[k : k + 1]
-        if padded != width:
-            row = jnp.concatenate([row, jnp.zeros((1, padded - width), f32)], axis=1)
-        send(msg, LANES + k * padded, row, devices)
+    base = 3 * count + span + 2 * halo
+    pieces = coarse_rows.shape[1] // depth
+    coarse_rows[...] = jnp.zeros_like(coarse_rows)
+    for bx in range(3):
+        for t in range(pieces):
+            for by, tile in enumerate(three(base + bx * pieces + t)):
+                low = (bx * 3 + by) * 3
+                coarse_rows[low : low + 3, t * depth : (t + 1) * depth] = tile[:3]
 
 
 def iterate(dims, level, layouts, coup, store, residual, half, root, center, moved, moved_next, z_all, image):
@@ -325,18 +397,13 @@
 
 
 def first_kernel(
-    dims, counts, where, coup, got, kh_w, h_w, v_w, root_w, kh_m, h_m, kh_o, v_o, root_o,
+    dims, coup, got, coarse_rows, kh_w, h_w, v_w, root_w, kh_m, h_m, kh_o, v_o, root_o,
     z_own, mapped, msg,
     moved, moved_next, moved_own, z_all, store, sums,
 ):
     span, depth, devices = dims
     level = REACH
-    padded = (got.shape[2] - LANES) // 3
-    coarse_values(
-        got[:, 0, :LANES],
-        lambda k: got[:, 0, LANES + k * padded : LANES + (k + 1) * padded],
-        where, counts, store,
-    )
+    coarse_values(got[:, 0], coarse_rows, store)
 
     def image(x):
         out, _ = stencil(moved_next, x + 1, coup, lambda i, cut: kh_m[i, x, :, cut])
@@ -376,7 +443,7 @@
 
 
 def second_kernel(
-    dims, counts, where, coup, got, first, kh_m, h_m, v_m, root_m, kh_o, root_o, mapped_old,
+    dims, coup, got, first, coarse_rows, kh_m, h_m, v_m, root_m, kh_o, root_o, mapped_old,
     z_own, mapped, residual, means, msg,
     moved, moved_next, moved_own, z_all, store, sums,
 ):
@@ -385,14 +452,9 @@
     total = row_sum(got[:, 0])
     gamma = pick(total, 3)
     step = gamma / pick(total, 4)
-    padded = (first.shape[2] - LANES) // 3
-    fresh = first[:, 0, :LANES] - step * got[:, 0]
+    fresh = first[:, 0] - step * got[:, 0]
     means[...] = fresh
-    coarse_values(
-        fresh,
-        lambda k: first[:, 0, LANES + k * padded : LANES + (k + 1) * padded],
-        where, counts, store,
-    )
+    coarse_values(fresh, coarse_rows, store)
     size = scalar(step)
 
     def rest(k, x):
@@ -442,7 +504,7 @@
 
 
 def third_kernel(
-    dims, counts, where, coup, got, got_old, first, means, kh_m, h_m, root_m, kh_o, v_o, root_o,
+    dims, coup, got, got_old, means, coarse_rows, kh_m, h_m, root_m, kh_o, v_o, root_o,
     z_old, mapped_old, z_new, mapped_new, residual_old, lanczos, previous, locked,
     base, z_out, dir_out, scal, msg,
     moved, moved_next, residual, mapped, z_all, store, sums, locked_sums,
@@ -459,12 +521,7 @@
     delta = pick(total, 4) + 2.0 * ratio * pick(total, 5) + ratio * ratio * delta_old
     step = gamma / delta
     fresh = means[...] - step * (got[:, 0] + ratio * got_old[:, 0])
-    padded = (first.shape[2] - LANES) // 3
-    coarse_values(
-        fresh,
-        lambda k: first[:, 0, LANES + k * padded : LANES + (k + 1) * padded],
-        where, counts, store,
-    )
+    coarse_values(fresh, coarse_rows, store)
     lane = lax.broadcasted_iota(jnp.int32, (1, LANES), 1)
     scal[...] = jnp.where(lane == 0, gamma, jnp.where(lane == 1, delta, 0.0))
     size, size_old, blend = scalar(step), scalar(step_old), scalar(ratio)
@@ -581,14 +638,20 @@
 
 VMEM = pl.BlockSpec(memory_space=pltpu.VMEM)
 SMEM = pl.BlockSpec(memory_space=pltpu.SMEM)
-
-
-def call(kernel, name, outs, scratch, *operands, limit=60 << 20):
+HBM = pl.BlockSpec(memory_space=pltpu.HBM)
+
+
+def call(kernel, name, outs, scratch, *operands, limit, stay=0):
+    places = [SMEM if len(operand.shape) == 1 else VMEM for operand in operands]
+    if stay:
+        places[-stay:] = [HBM] * stay
+        kept = [pltpu.with_memory_space_constraint(operand, pltpu.HBM) for operand in operands[-stay:]]
+        operands = (*operands[:-stay], *kept)
     return pl.pallas_call(
         kernel,
         name=name,
         out_shape=[jax.ShapeDtypeStruct(shape, f32) for shape in outs],
-        in_specs=[SMEM if len(operand.shape) == 1 else VMEM for operand in operands],
+        in_specs=places,
         out_specs=[SMEM if len(shape) == 1 else VMEM for shape in outs],
         scratch_shapes=scratch,
         compiler_params=pltpu.CompilerParams(vmem_limit_bytes=limit),
@@ -624,41 +687,43 @@
     groups = jnp.stack([flat, 0.5 * (up + down), 0.5 * (up - down)], axis=1)
     coup = jnp.concatenate([groups.reshape(-1), six[12], previous_beta.reshape(1)])
 
-    density = jnp.where(occupancy == 1, 1.0, VOID_DENSITY).astype(f32)
-    density = jnp.repeat(jnp.repeat(jnp.repeat(density, BRICK, 0), BRICK, 1), BRICK, 2)
-    stiffness = density * young
-    fields = jnp.concatenate([lanczos_vector, stiffness[None]], axis=0)
-
-    odd = slab % 2
-    near, far = swap_permutes("slab")
-    upper = lax.slice_in_dim(fields, span - halo, span, axis=1)
-    lower = lax.slice_in_dim(fields, 0, halo, axis=1)
-    from_near = lax.ppermute(jnp.where(odd == 0, upper, lower), "slab", near)
-    from_far = lax.ppermute(jnp.where(odd == 0, lower, upper), "slab", far)
-    below = jnp.where(odd == 0, from_far, from_near)
-    above = jnp.where(odd == 0, from_near, from_far)
-    tall = jnp.concatenate([below, fields, above], axis=1)
-    near, far = swap_permutes("block")
-    tall, where, coup, coarse_inverse = lax.optimization_barrier((tall, where, coup, coarse_inverse))
-    side_near = lax.ppermute(tall, "block", near)
-    side_far = lax.ppermute(tall, "block", far)
-
     dims = (span, depth, devices)
+    pieces = -(-coarse_inverse.shape[1] // depth)
+    own = (3, span, 8, depth)
+
+    def scratch(*shape):
+        return pltpu.VMEM(shape, f32)
+
+    tiles = (3 * REACH + halo + pieces, 8, depth)
+    near, far, vector, stiff, coarse = call(
+        functools.partial(pack_kernel, dims),
+        "pack",
+        [tiles, tiles, own, own[1:], (pieces, 8, depth)],
+        [scratch(*own[1:]), scratch(*coarse_inverse.shape), pltpu.SemaphoreType.DMA((3,))],
+        where, pltpu.with_memory_space_constraint(occupancy.reshape(-1), pltpu.HBM), lanczos_vector, young, coarse_inverse, limit=6 << 20, stay=3,
+    )
+    to_near, to_far = swap_permutes("slab")
+    near, far = lax.ppermute(near, "slab", to_near), lax.ppermute(far, "slab", to_far)
+    (tall,) = call(
+        functools.partial(tall_kernel, dims),
+        "tall",
+        [(3 * (span + 2 * REACH) + span + 2 * halo + 3 * pieces, 8, depth)],
+        [],
+        where, near, far, vector, stiff, coarse, limit=6 << 20,
+    )
+    to_near, to_far = swap_permutes("block")
+    tall, coup = lax.optimization_barrier((tall, coup))
+    side_near, side_far = lax.ppermute(tall, "block", to_near), lax.ppermute(tall, "block", to_far)
+
     wide = (span + 2 * REACH, WIDE[1], depth)
     mid = (span + 8, MID[1], depth)
-    own = (3, span, 8, depth)
-    padded = -(-coarse_inverse.shape[1] // LANES) * LANES
     row = (devices, 1, LANES)
-
-    def scratch(*shape):
-        return pltpu.VMEM(shape, f32)
-
-    kh_w, h_w, v_w, root_w, kh_m, h_m, v_m, root_m, kh_o, v_o, root_o, msg = call(
+    kh_w, h_w, v_w, root_w, kh_m, h_m, v_m, root_m, kh_o, v_o, root_o, rows, msg = call(
         functools.partial(setup_kernel, dims),
         "setup",
         [
             (6, *wide), (3, *wide), (3, *wide), wide, (6, *mid), (3, *mid), (3, *mid), mid,
-            (6, *own[1:]), own, own[1:], (devices, 1, LANES + 3 * padded),
+            (6, *own[1:]), own, own[1:], (32, pieces * depth), row,
         ],
         [
             scratch(3, span + 2 * halo + 1, WIDE[1], depth),
@@ -666,13 +731,13 @@
             scratch(9, span + 2, 8, depth),
             scratch(8, depth),
         ],
-        where, coup, side_near, side_far, tall, coarse_inverse, limit=9 << 20,
+        where, coup, side_near, side_far, tall, limit=9 << 20,
     )
     first = exchange_rows(msg)
 
     store = pltpu.SMEM((27,), f32)
     z_0, mapped_0, msg = call(
-        functools.partial(first_kernel, dims, counts),
+        functools.partial(first_kernel, dims),
         "first",
         [own, (3, *mid), row],
         [
@@ -683,14 +748,14 @@
             store,
             scratch(8, depth),
         ],
-        where, coup, first, kh_w, h_w, v_w, root_w, kh_m, h_m, kh_o, v_o, root_o, limit=28 << 20,
+        coup, first, rows, kh_w, h_w, v_w, root_w, kh_m, h_m, kh_o, v_o, root_o, limit=14 << 20,
     )
     got_0 = exchange_rows(msg)
 
     level = REACH - 2
     inner = (3, span + 2 * level - 4, MID[1], depth)
     z_1, mapped_1, residual, means, msg = call(
-        functools.partial(second_kernel, dims, counts),
+        functools.partial(second_kernel, dims),
         "second",
         [own, inner, inner, (devices, LANES), row],
         [
@@ -701,13 +766,13 @@
             store,
             scratch(8, depth),
         ],
-        where, coup, got_0, first, kh_m, h_m, v_m, root_m, kh_o, root_o, mapped_0, limit=18 << 20,
+        coup, got_0, first, rows, kh_m, h_m, v_m, root_m, kh_o, root_o, mapped_0, limit=10 << 20,
     )
     got_1 = exchange_rows(msg)
 
     level = REACH - 4
     base, z_2, direction, scal, msg = call(
-        functools.partial(third_kernel, dims, counts),
+        functools.partial(third_kernel, dims),
         "third",
         [own, own, own, (1, LANES), (devices, 1, 2 * LANES)],
         [
@@ -720,8 +785,8 @@
             scratch(8, depth),
             scratch(locked, 4, depth),
         ],
-        where, coup, got_1, got_0, first, means, kh_m, h_m, root_m, kh_o, v_o, root_o,
-        z_0, mapped_0, z_1, mapped_1, residual, lanczos_vector, previous_vector, locked_vectors, limit=16 << 20,
+        coup, got_1, got_0, means, rows, kh_m, h_m, root_m, kh_o, v_o, root_o,
+        z_0, mapped_0, z_1, mapped_1, residual, lanczos_vector, previous_vector, locked_vectors, limit=9 << 20,
     )
     got_2 = exchange_rows(msg)
 

time: 113 us -> 109 us (0.965)
  waiting for transfers between devices: 9.57 us -> 4.32 us
  blocking collectives: 54.7 us -> 59.3 us
  other arithmetic: 3.67 us -> 0.87 us
  Pallas kernels: 32 us -> 34.5 us
  starting transfers between devices: 10.1 us -> 7.86 us
    ppermute x4, waiting for transfers between devices: 9.57 us -> 4.32 us  [the longest x1 2.53 us: shards(): lax.ppermute(near, 'slab', to_near)]
    all_to_all x5, blocking collectives: 54.7 us -> 59.3 us  [exchange_rows(): return lax.all_to_all(rows, AXES, 0, 0, tiled=True)]
    pallas_call x6 -> x8, Pallas kernels: 32 us -> 34.5 us  [call(): pl.pallas_call(kernel, name=name, out_shape=[jax.ShapeDtypeStruct(shape,...]
    ppermute x4, starting transfers between devices: 10.1 us -> 7.86 us  [the longest x1 3.46 us: shards(): lax.ppermute(tall, 'block', to_near)]
    select_n x3 -> x0, other arithmetic: 1.9 us -> none  [the longest x1 1.18 us: shards(): from_far = lax.ppermute(jnp.where(odd == 0, lower, upper), 'slab', far)]
where the time goes in v4:
time: 109 us
  blocking collectives  59.3 us (54%)
  Pallas kernels  34.5 us (32%)
  starting transfers between devices  7.86 us (7%)
  waiting for transfers between devices  4.32 us (4%)
  between operations  1.38 us (1%)
    all_to_all x5, blocking collectives, exchange_rows(): return lax.all_to_all(rows, AXES, 0, 0, tiled=True)  59.3 us
    pallas_call x8, Pallas kernels, call(): pl.pallas_call(kernel, name=name, out_shape=[jax.ShapeDtypeStruct(shape,...  34.5 us
    ppermute x1, starting transfers between devices, shards(): lax.ppermute(tall, 'block', to_near)  3.46 us
    ppermute x1, starting transfers between devices, shards(): lax.ppermute(near, 'slab', to_near)  3.03 us
    ppermute x1, waiting for transfers between devices, shards(): lax.ppermute(near, 'slab', to_near)  2.53 us
  transfers between devices with their start and end apart: 4, of which 2 were waited for; matrix products, arithmetic and copies ran while one was open for 2% of the time, Pallas kernels for 0%

profile of v4, /device:TPU:0, one launch (start us, length us, event | category | flops | bytes accessed | tf_op | source)
XLA Modules:
  0.0 109.0 jit_solution(6329416817703249669)
XLA Ops:
  0.6 0.1 pad_add_fusion.where
  0.7 1.7 %pack.1 = (f32[26,8,256]{2,1,0:T(8,128)S(1)}, f32[26,8,256]{2,1,0:T(8,128)S(1)}, f32[3,8,8,256]{3,2,1,0:T(8,128)S(1)}, f32[8,8,256]{2,1,0:T(8,128)S(1)}, f32[1,8,256]{2,1,0:T(8,128)S(1)}) custom-call(s32[2]{0:T(128)S(1)} %pad_add_fusion.where, s32[32]{0:T(128)} %bitcast.13, f32[3,8,8,256]{3,2,1,0:T(8,128)} %lanczos.3, f32[8,8,256]{2,1,0:T(8,128)} %young_in.1, ...), custom_call_target="tpu_custom_call" | custom-call | tf_op jit(solution)/shard_map/pack/pallas_call | solution.py:650
  2.4 3.0 %collective-permute-start = (f32[26,8,256]{2,1,0:T(8,128)S(1)}, f32[26,8,256]{2,1,0:T(8,128)S(1)}, u32[]{:S(2)}, u32[]{:S(2)}) collective-permute-start(f32[26,8,256]{2,1,0:T(8,128)S(1)} %get-tuple-element.40), channel_id=1, source_target_pairs={{0,8},{8,0},{16,24},{24,16},{1,9},{9,1},{17,25},{25,17},{2,10},{10... | collective-permute-start | bytes 638984 | tf_op jit(solution)/shard_map/ppermute | solution.py:706
  5.5 0.7 collective-permute-start.1
  6.1 0.7 neg.6
  6.9 0.1 slice.42
  7.0 0.1 slice.41
  7.1 0.1 slice.40
  7.8 0.1 copy.15
  7.9 0.1 copy.16
  8.0 0.1 copy.17
  8.1 0.1 reshape.18
  8.2 0.2 slice_reduce_fusion
  8.4 0.1 pad_maximum_fusion.1.coup
  8.4 2.5 %collective-permute-done.near = f32[26,8,256]{2,1,0:T(8,128)S(1)} collective-permute-done((f32[26,8,256]{2,1,0:T(8,128)S(1)}, f32[26,8,256]{2,1,0:T(8,128)S(1)}, u32[]{:S(2)}, u32[]{:S(2)}) %collective-permute-start) | collective-permute-done | bytes 213024 | tf_op jit(solution)/shard_map/ppermute | solution.py:706
  11.0 0.0 collective-permute-done.1.far
  11.0 0.6 tall.1.mid
  11.6 0.7 collective-permute-start.3
  12.3 3.5 %collective-permute-start.2 = (f32[85,8,256]{2,1,0:T(8,128)S(1)}, f32[85,8,256]{2,1,0:T(8,128)S(1)}, u32[]{:S(2)}, u32[]{:S(2)}) collective-permute-start(f32[85,8,256]{2,1,0:T(8,128)S(1)} %tall.1.mid), channel_id=1, source_target_pairs={{0,1},{1,0},{2,3},{3,2},{4,5},{5,4},{6,7},{7,6},{8,9},{9,8},{10,11... | collective-permute-start | bytes 2088968 | tf_op jit(solution)/shard_map/ppermute | solution.py:716
  15.8 0.0 collective-permute-done.3.odd
  15.8 1.8 %collective-permute-done.2.even = f32[85,8,256]{2,1,0:T(8,128)S(1)} collective-permute-done((f32[85,8,256]{2,1,0:T(8,128)S(1)}, f32[85,8,256]{2,1,0:T(8,128)S(1)}, u32[]{:S(2)}, u32[]{:S(2)}) %collective-permute-start.2) | collective-permute-done | bytes 696352 | tf_op jit(solution)/shard_map/ppermute | solution.py:716
  17.5 6.2 %setup.1 = (f32[6,20,24,256]{3,2,1,0:T(8,128)S(1)}, f32[3,20,24,256]{3,2,1,0:T(8,128)S(1)}, f32[3,20,24,256]{3,2,1,0:T(8,128)S(1)}, f32[20,24,256]{2,1,0:T(8,128...) custom-call(s32[2]{0:T(128)S(1)} %pad_add_fusion.where, ...), custom_call_target="tpu_custom_call" | custom-call | tf_op jit(solution)/shard_map/setup/pallas_call | solution.py:650
  23.8 23.8 %all_to_all.25.got.first = f32[32,1,128]{2,1,0:T(1,128)S(1)} all-to-all(f32[32,1,128]{2,1,0:T(1,128)S(1)} %get-tuple-element.47), channel_id=1, replica_groups=mesh['slab'=4,'block'=8] {'slab','block'}, dimensions={0} | all-to-all | bytes 32768 | tf_op jit(solution)/shard_map/all_to_all | solution.py:669
  47.6 9.8 %first.1 = (f32[3,8,8,256]{3,2,1,0:T(8,128)S(1)}, f32[3,16,16,256]{3,2,1,0:T(8,128)S(1)}, f32[32,1,128]{2,1,0:T(1,128)S(1)}) custom-call(f32[79]{0:T(128)S(1)} %pad_maximum_fusion.1.coup, f32[32,1,128]{2,1,0:T(1,128)S(1)} %all_to_all.25.got.first, f32[32,256]{1,0:T(8,128)S(1)} %get-tuple-element.48.coarse_rows, ...), custom_call_target="tpu_custom_call" | custom-call | tf_op jit(solution)/shard_map/first/pallas_call | solution.py:650
  57.4 8.9 %all_to_all.26.got.got_old = f32[32,1,128]{2,1,0:T(1,128)S(1)} all-to-all(f32[32,1,128]{2,1,0:T(1,128)S(1)} %get-tuple-element.58), channel_id=1, replica_groups=mesh['slab'=4,'block'=8] {'slab','block'}, dimensions={0} | all-to-all | bytes 32768 | tf_op jit(solution)/shard_map/all_to_all | solution.py:669
  66.2 0.0 copy-start
  66.2 0.0 copy-start.1
  66.2 0.0 copy-start.2
  66.2 7.5 %second.1 = (f32[3,8,8,256]{3,2,1,0:T(8,128)S(1)}, f32[3,12,16,256]{3,2,1,0:T(8,128)S(1)}, f32[3,12,16,256]{3,2,1,0:T(8,128)S(1)}, f32[32,128]{1,0:T(8,128)S(1)}, f32[32,1,128]{2,1,0:T(1,128)S(1)}) custom-call(f32[79]{0:T(128)S(1)} %pad_maximum_fusion.1.coup, f32[32,1,128]{2,1,0:T(1,128)S(1)} %all_to_all.26.got.got_old, ...), custom_call_target="tpu_custom_call" | custom-call | tf_op jit(solution)/shard_map/second/pallas_call | solution.py:650
  73.7 8.9 %all_to_all.27.got = f32[32,1,128]{2,1,0:T(1,128)S(1)} all-to-all(f32[32,1,128]{2,1,0:T(1,128)S(1)} %get-tuple-element.62), channel_id=1, replica_groups=mesh['slab'=4,'block'=8] {'slab','block'}, dimensions={0} | all-to-all | bytes 32768 | tf_op jit(solution)/shard_map/all_to_all | solution.py:669
  82.6 0.0 copy-done
  82.6 0.0 copy-done.1
  82.6 0.0 copy-done.2
  82.6 6.0 %third.1 = (f32[3,8,8,256]{3,2,1,0:T(8,128)S(1)}, f32[3,8,8,256]{3,2,1,0:T(8,128)S(1)}, f32[3,8,8,256]{3,2,1,0:T(8,128)S(1)}, f32[1,128]{1,0:T(1,128)S(1)}, f32[32,1,256]{2,1,0:T(1,128)S(1)}) custom-call(f32[79]{0:T(128)S(1)} %pad_maximum_fusion.1.coup, f32[32,1,128]{2,1,0:T(1,128)S(1)} %all_to_all.27.got, f32[32,1,128]{2,1,0:T(1,128)S(1)} %all_to_all.26.got.got_old, ...), custom_call_target="tpu_custom_call" | custom-call | tf_op jit(solution)/shard_map/third/pallas_call | solution.py:650
  88.6 8.9 %all_to_all.28.got = f32[32,1,256]{2,1,0:T(1,128)S(1)} all-to-all(f32[32,1,256]{2,1,0:T(1,128)S(1)} %get-tuple-element.68), channel_id=1, replica_groups=mesh['slab'=4,'block'=8] {'slab','block'}, dimensions={0} | all-to-all | bytes 65536 | tf_op jit(solution)/shard_map/all_to_all | solution.py:669
  97.5 1.3 %last.1 = (f32[3,8,8,256]{3,2,1,0:T(8,128)}, f32[16]{0:T(128)}, f32[1]{0:T(128)}, f32[32,1,128]{2,1,0:T(1,128)S(1)}) custom-call(f32[32,1,256]{2,1,0:T(1,128)S(1)} %all_to_all.28.got, f32[1,128]{1,0:T(1,128)S(1)} %get-tuple-element.69.scal, f32[3,8,8,256]{3,2,1,0:T(8,128)S(1)} %get-tuple-element.70.base, f32[3,8,8,256]{3,2,1,0:T(8,128)S(1)} %get-tuple-element.71.z, ...), custom_call_target="tpu_custom_call" | custom-call | tf_op jit(solution)/shard_map/last/pallas_call | solution.py:650
  98.9 8.9 %all_to_all.29.got = f32[32,1,128]{2,1,0:T(1,128)S(1)} all-to-all(f32[32,1,128]{2,1,0:T(1,128)S(1)} %get-tuple-element.74), channel_id=1, replica_groups=mesh['slab'=4,'block'=8] {'slab','block'}, dimensions={0} | all-to-all | bytes 32768 | tf_op jit(solution)/shard_map/all_to_all | solution.py:669
  107.8 1.3 %closing.1 = f32[2]{0:T(128)} custom-call(f32[32,1,128]{2,1,0:T(1,128)S(1)} %all_to_all.29.got, f32[1]{0:T(128)} %get-tuple-element.75.found), custom_call_target="tpu_custom_call" | custom-call | tf_op jit(solution)/shard_map/closing/pallas_call | solution.py:650
  (7 shorter events, 0.1 us)
Async XLA Ops:
  2.4 8.5 %collective-permute-start = (f32[26,8,256]{2,1,0:T(8,128)S(1)}, f32[26,8,256]{2,1,0:T(8,128)S(1)}, u32[]{:S(2)}, u32[]{:S(2)}) collective-permute-start(f32[26,8,256]{2,1,0:T(8,128)S(1)} %get-tuple-element.40), channel_id=1, source_target_pairs={{0,8},{8,0},{16,24},{24,16},{1,9},{9,1},{17,25},{25,17},{2,10},{10... | collective-permute-start | bytes 638984 | tf_op jit(solution)/shard_map/ppermute | solution.py:706
  5.5 5.5 %collective-permute-start.1 = (f32[26,8,256]{2,1,0:T(8,128)S(1)}, f32[26,8,256]{2,1,0:T(8,128)S(1)}, u32[]{:S(2)}, u32[]{:S(2)}) collective-permute-start(f32[26,8,256]{2,1,0:T(8,128)S(1)} %get-tuple-element.41), channel_id=1, source_target_pairs={{8,16},{16,8},{9,17},{17,9},{10,18},{18,10},{11,19},{19,11},{12,20... | collective-permute-start | bytes 638984 | tf_op jit(solution)/shard_map/ppermute | solution.py:706
  11.6 4.2 %collective-permute-start.3 = (f32[85,8,256]{2,1,0:T(8,128)S(1)}, f32[85,8,256]{2,1,0:T(8,128)S(1)}, u32[]{:S(2)}, u32[]{:S(2)}) collective-permute-start(f32[85,8,256]{2,1,0:T(8,128)S(1)} %tall.1.mid), channel_id=1, source_target_pairs={{1,2},{2,1},{3,4},{4,3},{5,6},{6,5},{9,10},{10,9},{11,12},{12,11},... | collective-permute-start | bytes 2088968 | tf_op jit(solution)/shard_map/ppermute | solution.py:716
  12.3 5.2 %collective-permute-start.2 = (f32[85,8,256]{2,1,0:T(8,128)S(1)}, f32[85,8,256]{2,1,0:T(8,128)S(1)}, u32[]{:S(2)}, u32[]{:S(2)}) collective-permute-start(f32[85,8,256]{2,1,0:T(8,128)S(1)} %tall.1.mid), channel_id=1, source_target_pairs={{0,1},{1,0},{2,3},{3,2},{4,5},{5,4},{6,7},{7,6},{8,9},{9,8},{10,11... | collective-permute-start | bytes 2088968 | tf_op jit(solution)/shard_map/ppermute | solution.py:716
  66.2 16.4 %copy-start = (f32[16,3,8,8,256]{4,3,2,1,0:T(8,128)S(1)}, f32[16,3,8,8,256]{4,3,2,1,0:T(8,128)}, u32[]{:S(2)}) copy-start(f32[16,3,8,8,256]{4,3,2,1,0:T(8,128)} %locked.3) | copy-start | bytes 9437188
  66.2 16.4 %copy-start.1 = (f32[3,8,8,256]{3,2,1,0:T(8,128)S(1)}, f32[3,8,8,256]{3,2,1,0:T(8,128)}, u32[]{:S(2)}) copy-start(f32[3,8,8,256]{3,2,1,0:T(8,128)} %lanczos.3) | copy-start | bytes 589828
  66.2 16.4 %copy-start.2 = (f32[3,8,8,256]{3,2,1,0:T(8,128)S(1)}, f32[3,8,8,256]{3,2,1,0:T(8,128)}, u32[]{:S(2)}) copy-start(f32[3,8,8,256]{3,2,1,0:T(8,128)} %previous.1) | copy-start | bytes 589828
